TPU v7x, 128 devices: a whole 4x4x4 slice. The times are simulated.
128 devices in a mesh: dp: 8 (over x, y_lo), expert: 16 (over z, y_hi, core).
Axes of the slice: x: 4, y: 4 (y_hi: 2, y_lo: 2; y = y_hi * 2 + y_lo), z: 4, core: 2. Of those that a mesh axis runs over, the one named last changes fastest.
Arguments:
- tokens: bfloat16 [32768, 1536], P(('dp', 'expert')), may hold values from -24 to 24
- cotangent: bfloat16 [32768, 1536], P(('dp', 'expert')), may hold values from -0.59765625 to 0.59765625
- chosen: int32 [512, 16, 8], P(('dp', 'expert')), may hold values from 0 to 63, as said below
- w_router: bfloat16 [1536, 16], replicated, may hold values from -0.15625 to 0.15625
- w_gate: bfloat16 [16, 1536, 1024], P('expert', 'dp'), may hold values from -0.15625 to 0.15625
- w_up: bfloat16 [16, 1536, 1024], P('expert', 'dp'), may hold values from -0.15625 to 0.15625
- w_down: bfloat16 [16, 1024, 1536], P('expert', 'dp'), may hold values from -0.1875 to 0.1875
Outputs:
- mixed: bfloat16 [32768, 1536], P(('dp', 'expert'))
- grad_tokens: bfloat16 [32768, 1536], P(('dp', 'expert'))
- grad_gate: float32 [16, 1536, 1024], P('expert', 'dp')
- grad_up: float32 [16, 1536, 1024], P('expert', 'dp')
- down_weight_gradient: float32 [16, 1024, 1536], P('expert', 'dp')
- grad_router: float32 [1536, 16], replicated
Inputs may be any that keep to these rules, and one draw needn't show every extreme that they name: `chosen`: for each aligned block of 64 token rows and each expert, 8 different row numbers within the block; so every device has exactly 32 slots for each expert.
All inputs are finite; a program needn't handle non-finite values.
Results may differ from a plain program's by a relative error of at most 0.017.
Values may be sent and summed in bfloat16 or wider, within the bound.
A program may use at most 128 MiB of HBM per device.

v0:
```python
import jax
import jax.numpy as jnp
from jax import lax
from jax.sharding import PartitionSpec as P


def to_blocks(slot_array, num_blocks, pick_count):
    expert_count = slot_array.shape[0]
    trailing = slot_array.shape[2:]
    grouped = slot_array.reshape((expert_count, num_blocks, pick_count) + trailing)
    axis_order = (1, 0, 2) + tuple(range(3, 3 + len(trailing)))
    return jnp.transpose(grouped, axis_order).reshape(
        (num_blocks, expert_count * pick_count) + trailing
    )


def weight_grads(expert_rows, hidden, expert_cot, d_pre_gate, d_pre_up):
    hidden_activations = hidden.shape[2]
    both_grads = jnp.concatenate([d_pre_gate, d_pre_up], axis=2)
    columns = expert_rows
    in_share = lax.psum_scatter(
        jnp.einsum("erc,erk->cek", columns, both_grads, preferred_element_type=jnp.float32).astype(
            jnp.bfloat16
        ),
        "dp",
        scatter_dimension=0,
        tiled=True,
    ).astype(jnp.float32)
    grad_gate = jnp.transpose(in_share[:, :, :hidden_activations], (1, 0, 2))
    grad_up = jnp.transpose(in_share[:, :, hidden_activations:], (1, 0, 2))
    columns = hidden
    out_share = lax.psum_scatter(
        jnp.einsum("erc,erd->ced", columns, expert_cot, preferred_element_type=jnp.float32).astype(
            jnp.bfloat16
        ),
        "dp",
        scatter_dimension=0,
        tiled=True,
    ).astype(jnp.float32)
    down_weight_gradient = jnp.transpose(out_share, (1, 0, 2))
    return (grad_gate, grad_up, down_weight_gradient)


def body(tokens, cotangent, chosen, w_router, w_gate, w_up, w_down):
    tok_rows, model_width = tokens.shape
    num_blocks, expert_count, pick_count = chosen.shape
    block_rows = tok_rows // num_blocks
    slot_count = num_blocks * pick_count
    logits = jnp.dot(tokens, w_router, preferred_element_type=jnp.float32)
    gate_values = jax.nn.sigmoid(logits)
    offsets = (jnp.arange(num_blocks, dtype=jnp.int32) * block_rows)[:, None, None]
    slot_rows = jnp.transpose(chosen + offsets, (1, 0, 2)).reshape(expert_count, slot_count)
    picked = tokens[slot_rows]
    slot_gate_values = jnp.take_along_axis(gate_values.T, slot_rows, axis=1)
    cot_rows = cotangent[slot_rows]
    scaled_cot = (slot_gate_values[:, :, None] * cot_rows.astype(jnp.float32)).astype(jnp.bfloat16)
    full_gate, full_up, full_down = (
        lax.all_gather(w_gate, "dp", axis=1, tiled=True),
        lax.all_gather(w_up, "dp", axis=1, tiled=True),
        lax.all_gather(w_down, "dp", axis=1, tiled=True),
    )
    expert_rows = lax.all_to_all(picked, "expert", split_axis=0, concat_axis=1, tiled=True)
    pre_gate = jnp.einsum(
        "erd,edh->erh", expert_rows, full_gate, preferred_element_type=jnp.float32
    )
    pre_up = jnp.einsum("erd,edh->erh", expert_rows, full_up, preferred_element_type=jnp.float32)
    silu_gate = jax.nn.silu(pre_gate)
    hidden = (silu_gate * pre_up).astype(jnp.bfloat16)
    expert_out = jnp.einsum(
        "erh,ehd->erd", hidden, full_down, preferred_element_type=jnp.float32
    ).astype(jnp.bfloat16)
    returned = lax.all_to_all(expert_out, "expert", split_axis=1, concat_axis=0, tiled=True)
    expert_cot = lax.all_to_all(scaled_cot, "expert", split_axis=0, concat_axis=1, tiled=True)
    back_gate, back_up, back_down = (full_gate, full_up, full_down)
    d_hidden = jnp.einsum("erd,ehd->erh", expert_cot, back_down, preferred_element_type=jnp.float32)
    gate_sigmoid = jax.nn.sigmoid(pre_gate)
    d_pre_gate = (
        d_hidden * pre_up * gate_sigmoid * (1.0 + pre_gate * (1.0 - gate_sigmoid))
    ).astype(jnp.bfloat16)
    d_pre_up = (d_hidden * silu_gate).astype(jnp.bfloat16)
    d_rows = (
        jnp.einsum("erh,edh->erd", d_pre_gate, back_gate, preferred_element_type=jnp.float32)
        + jnp.einsum("erh,edh->erd", d_pre_up, back_up, preferred_element_type=jnp.float32)
    ).astype(jnp.bfloat16)
    row_grads = lax.all_to_all(d_rows, "expert", split_axis=1, concat_axis=0, tiled=True)
    position_hits = chosen[:, :, :, None] == jnp.arange(block_rows, dtype=jnp.int32)
    indicator_matrix = position_hits.reshape(num_blocks, expert_count * pick_count, block_rows)
    gate_weighted_rows = to_blocks(slot_gate_values, num_blocks, pick_count)[
        :, :, None
    ] * to_blocks(returned, num_blocks, pick_count).astype(jnp.float32)
    mixed = (
        jnp.einsum(
            "wze,wzi->wei",
            indicator_matrix.astype(jnp.float32),
            gate_weighted_rows,
            precision=lax.Precision.HIGHEST,
        )
        .reshape(tok_rows, model_width)
        .astype(jnp.bfloat16)
    )
    slot_dots = jnp.sum(cot_rows.astype(jnp.float32) * returned.astype(jnp.float32), axis=2)
    dgate = jnp.einsum(
        "bept,ebp->bte",
        position_hits.astype(jnp.float32),
        slot_dots.reshape(expert_count, num_blocks, pick_count),
        precision=lax.Precision.HIGHEST,
    ).reshape(tok_rows, expert_count)
    d_logit = (dgate * gate_values * (1.0 - gate_values)).astype(jnp.bfloat16)
    gathered_grads = jnp.einsum(
        "wze,wzi->wei",
        indicator_matrix.astype(jnp.bfloat16),
        to_blocks(row_grads, num_blocks, pick_count),
        preferred_element_type=jnp.float32,
    ).reshape(tok_rows, model_width)
    grad_tokens = (
        gathered_grads + jnp.dot(d_logit, w_router.T, preferred_element_type=jnp.float32)
    ).astype(jnp.bfloat16)
    grad_router = lax.psum(
        jnp.dot(tokens.T, d_logit, preferred_element_type=jnp.float32), ("dp", "expert")
    )
    grad_gate, grad_up, down_weight_gradient = weight_grads(
        expert_rows, hidden, expert_cot, d_pre_gate, d_pre_up
    )
    return (mixed, grad_tokens, grad_gate, grad_up, down_weight_gradient, grad_router)


def solution(mesh):
    placed = (
        P(("dp", "expert"), None),
        P(("dp", "expert"), None),
        P(("dp", "expert"), None, None),
        P(),
        P("expert", "dp", None),
        P("expert", "dp", None),
        P("expert", "dp", None),
    )
    return jax.shard_map(
        body,
        mesh=mesh,
        in_specs=placed,
        out_specs=(
            P(("dp", "expert"), None),
            P(("dp", "expert"), None),
            P("expert", "dp", None),
            P("expert", "dp", None),
            P("expert", "dp", None),
            P(),
        ),
        check_vma=False,
    )
```

profile of v0, /device:TPU:5, one launch (start us, length us, event | category | flops | bytes accessed | tf_op | source)
XLA Modules:
  0.0 654.0 jit_solution(1444224585253242615)
XLA Ops:
  10.4 2.9 gather_fusion
  13.3 8.8 %all-to-all-start = ((bf16[16,32,1536]{2,1,0:T(8,128)(2,1)}), bf16[16,32,1536]{2,1,0:T(8,128)(2,1)}, u32[]{:S(2)}, u32[]{:S(2)}) async-start(bf16[16,32,1536]{2,1,0:T(8,128)(2,1)} %bitcast.5), calls=%async_computation | async-start | bytes 3145728 | tf_op jit(solution)/shard_map/all_to_all | solution.py:62
  22.6 4.5 gather_fusion.2
  31.1 49.5 %all-to-all-done = bf16[16,32,1536]{2,1,0:T(8,128)(2,1)} async-done(((bf16[16,32,1536]{2,1,0:T(8,128)(2,1)}), bf16[16,32,1536]{2,1,0:T(8,128)(2,1)}, u32[]{:S(2)}, u32[]{:S(2)}) %all-to-all-start) | async-done | bytes 1572896 | tf_op jit(solution)/shard_map/all_to_all | solution.py:62
  80.6 4.5 all-to-all-start.2
  85.2 22.3 %all-gather.4.cloned.1.call-done = bf16[1,1536,1024]{2,1,0:T(8,128)(2,1)} async-done(((bf16[1,192,1024]{2,1,0:T(8,128)(2,1)}), bf16[1,1536,1024]{2,1,0:T(8,128)(2,1)}) %all-gather.4.cloned.1.call-update) | async-done | bytes 3145744 | tf_op jit(solution)/shard_map/all_gather | solution.py:58
  107.5 5.5 fusion.13
  113.0 67.9 %all-gather.6.cloned.1.call-done = bf16[1,1536,1024]{2,1,0:T(8,128)(2,1)} async-done(((bf16[1,192,1024]{2,1,0:T(8,128)(2,1)}), bf16[1,1536,1024]{2,1,0:T(8,128)(2,1)}) %all-gather.6.cloned.1.call-update) | async-done | bytes 3145744 | tf_op jit(solution)/shard_map/all_gather | solution.py:59
  180.9 5.5 fusion.9
  186.4 67.4 %all-gather.8.cloned.1.call-done = bf16[1,1024,1536]{2,1,0:T(8,128)(2,1)} async-done(((bf16[1,128,1536]{2,1,0:T(8,128)(2,1)}), bf16[1,1024,1536]{2,1,0:T(8,128)(2,1)}) %all-gather.8.cloned.1.call-update) | async-done | bytes 3145744 | tf_op jit(solution)/shard_map/all_gather | solution.py:60
  253.8 7.4 %multiply_convert_fusion.1 = (bf16[512,1024]{1,0:T(8,128)(2,1)}, bf16[512,1024]{1,0:T(8,128)(2,1)}, bf16[512,1024]{1,0:T(8,128)(2,1)S(1)}) fusion(f32[512,1024]{1,0:T(8,128)} %fusion.13, f32[512,1024]{1,0:T(8,128)} %fusion.9, bf16[512,1536]{1,0:T(8,128)(2,1)} %bitcast.18, bf16[1,1024,1536]{2,1,0:T(8,128)(2,1)} %all-gather.8.cloned.1.call-done), kind=kOutput, calls=%fused_computation.36 | convolution fusion | flops 1618477056 | bytes 12058624 | tf_op jit(solution)/shard_map/erd,ehd->erh/dot_general | solution.py:75
  262.2 4.9 fusion.1
  267.2 4.7 copy.104
  272.1 8.1 %fusion = bf16[1536,2048]{0,1:T(8,128)(2,1)} fusion(bf16[512,1536]{1,0:T(8,128)(2,1)} %bitcast.6, bf16[1,512,1024]{2,1,0:T(8,128)(2,1)} %bitcast.148, bf16[1,512,1024]{2,1,0:T(8,128)(2,1)} %bitcast.149), kind=kOutput, calls=%fused_computation.4 | convolution fusion | flops 3228565504 | bytes 9961472 | tf_op jit(solution)/shard_map/erc,erk->cek/dot_general | solution.py:22
  280.3 8.9 %copy.102 = bf16[1536,2048]{1,0:T(8,128)(2,1)} copy(bf16[1536,2048]{0,1:T(8,128)(2,1)} %fusion) | data formatting | bytes 12582912
  289.2 4.2 fusion.11
  295.3 4.1 copy.126
  300.0 12.8 %reduce.2 = bf16[512,1536]{1,0:T(8,128)(2,1)} reduce(bf16[512,1,1536]{2,1,0:T(2,128)(2,1)} %bitcast.140, bf16[]{:T(256)} %broadcast.103), dimensions={1}, to_apply=%bitcast.134.reduce_sub_computation | reduce | bytes 3145730
  312.7 5.0 reshape.248
  317.7 5.9 all-to-all-start.3
  323.6 4.0 fusion.25
  327.6 4.1 copy.127
  331.8 12.6 %reduce.1 = bf16[512,1536]{1,0:T(8,128)(2,1)} reduce(bf16[512,1,1536]{2,1,0:T(2,128)(2,1)} %bitcast.142, bf16[]{:T(256)} %broadcast.103), dimensions={1}, to_apply=%bitcast.135.reduce_sub_computation | reduce | bytes 3145730
  344.4 5.0 reshape.246
  349.3 13.2 %all-to-all-done.3 = bf16[16,2,24576]{2,1,0:T(2,128)(2,1)} async-done(((bf16[16,2,24576]{2,1,0:T(2,128)(2,1)}), bf16[16,2,24576]{2,1,0:T(2,128)(2,1)}, u32[]{:S(2)}, u32[]{:S(2)}) %all-to-all-start.3) | async-done | bytes 1572896 | tf_op jit(solution)/shard_map/all_to_all | solution.py:85
  362.5 4.6 all-to-all-start.1
  367.8 10.0 %reshape.249 = bf16[512,1,1536]{2,1,0:T(2,128)(2,1)} reshape(bf16[16,2,24576]{2,1,0:T(2,128)(2,1)} %all-to-all-done.3) | data formatting | bytes 3145728
  377.8 3.4 copy.106
  381.2 46.3 %all-to-all-done.1 = bf16[16,2,24576]{2,1,0:T(2,128)(2,1)} async-done(((bf16[16,2,24576]{2,1,0:T(2,128)(2,1)}), bf16[16,2,24576]{2,1,0:T(2,128)(2,1)}, u32[]{:S(2)}, u32[]{:S(2)}) %all-to-all-start.1) | async-done | bytes 1572896 | tf_op jit(solution)/shard_map/all_to_all | solution.py:72
  427.5 10.0 %reshape.247 = bf16[512,1,1536]{2,1,0:T(2,128)(2,1)} reshape(bf16[16,2,24576]{2,1,0:T(2,128)(2,1)} %all-to-all-done.1) | data formatting | bytes 3145728
  448.9 53.1 %reduce-scatter.7.cloned.1.call-done = bf16[192,2048]{1,0:T(8,128)(2,1)} async-done(((bf16[1536,2048]{1,0:T(8,128)(2,1)}), bf16[192,2048]{1,0:T(8,128)(2,1)}) %reduce-scatter.7.cloned.1.call-update) | async-done | bytes 786448
  506.1 139.3 %all-reduce.2.cloned.1.call-done = f32[1536,16]{0,1:T(8,128)} async-done(((f32[1536,16]{0,1:T(8,128)}), f32[1536,16]{0,1:T(8,128)}) %all-reduce.2.cloned.1.call-update) | async-done | bytes 98320 | tf_op jit(solution)/shard_map/psum | solution.py:118
  (75 shorter events, 28.9 us)
Async XLA Ops:
  7.2 3.2 copy-start
  7.2 100.4 %all-gather.4.cloned.1.call-start = ((), (), s32[]{:S(2)}) async-start(), calls=%async_computation.6 | async-start | bytes 3538944 | tf_op jit(solution)/shard_map/all_gather | solution.py:58
  7.9 173.0 %all-gather.6.cloned.1.call-start = ((), (), s32[]{:S(2)}) async-start(), calls=%async_computation.7 | async-start | bytes 3538944 | tf_op jit(solution)/shard_map/all_gather | solution.py:59
  8.7 245.1 %all-gather.8.cloned.1.call-start = ((), (), s32[]{:S(2)}) async-start(), calls=%async_computation.8 | async-start | bytes 3538944 | tf_op jit(solution)/shard_map/all_gather | solution.py:60
  13.3 8.9 %copy-start.5 = (bf16[1536,16]{0,1:T(8,128)(2,1)S(1)}, bf16[1536,16]{0,1:T(8,128)(2,1)}, u32[]{:S(2)}) copy-start(bf16[1536,16]{0,1:T(8,128)(2,1)} %param.10) | copy-start | bytes 147460
  13.3 67.3 %all-to-all-start = ((bf16[16,32,1536]{2,1,0:T(8,128)(2,1)}), bf16[16,32,1536]{2,1,0:T(8,128)(2,1)}, u32[]{:S(2)}, u32[]{:S(2)}) async-start(bf16[16,32,1536]{2,1,0:T(8,128)(2,1)} %bitcast.5), calls=%async_computation | async-start | bytes 3145728 | tf_op jit(solution)/shard_map/all_to_all | solution.py:62
  22.6 4.7 copy-start.4
  22.6 4.8 copy-start.1
  80.6 105.8 %all-to-all-start.2 = ((bf16[16,32,1536]{2,1,0:T(8,128)(2,1)}), bf16[16,32,1536]{2,1,0:T(8,128)(2,1)}, u32[]{:S(2)}, u32[]{:S(2)}) async-start(bf16[16,32,1536]{2,1,0:T(8,128)(2,1)} %multiply_convert_fusion), calls=%async_computation.2 | async-start | bytes 3145728 | tf_op jit(solution)/shard_map/all_to_all | solution.py:73
  85.1 361.3 %reduce-scatter.9.cloned.1.call-start = ((), (), s32[]{:S(2)}) async-start(), calls=%async_computation.11 | async-start | bytes 3538944
  261.2 1.1 copy-start.8
  271.9 230.0 %reduce-scatter.7.cloned.1.call-start = ((), (), s32[]{:S(2)}) async-start(), calls=%async_computation.10 | async-start | bytes 7077888
  289.2 4.3 copy-start.6
  289.2 4.3 copy-start.7
  317.7 44.8 %all-to-all-start.3 = ((bf16[16,2,24576]{2,1,0:T(2,128)(2,1)}), bf16[16,2,24576]{2,1,0:T(2,128)(2,1)}, u32[]{:S(2)}, u32[]{:S(2)}) async-start(bf16[16,2,24576]{2,1,0:T(2,128)(2,1)} %reshape.248), calls=%async_computation.3 | async-start | bytes 3145728 | tf_op jit(solution)/shard_map/all_to_all | solution.py:85
  362.5 64.9 %all-to-all-start.1 = ((bf16[16,2,24576]{2,1,0:T(2,128)(2,1)}), bf16[16,2,24576]{2,1,0:T(2,128)(2,1)}, u32[]{:S(2)}, u32[]{:S(2)}) async-start(bf16[16,2,24576]{2,1,0:T(2,128)(2,1)} %reshape.246), calls=%async_computation.1 | async-start | bytes 3145728 | tf_op jit(solution)/shard_map/all_to_all | solution.py:72
  367.1 278.3 %all-reduce.2.cloned.1.call-start = ((), (), s32[]{:S(2)}) async-start(), calls=%async_computation.9 | async-start | bytes 196608 | tf_op jit(solution)/shard_map/psum | solution.py:118
  440.0 1.5 copy-start.3
  441.5 2.2 copy-start.2
Sparse Core Ops, SparseCore 0:
  9.7 97.8 all-gather.3
  109.2 71.7 all-gather.5
  182.6 71.1 all-gather.7
  272.0 78.7 reduce-scatter.8
  353.0 148.8 reduce-scatter.6
  507.1 138.2 all-reduce.1
where the time goes:
time: 665 us; the launch traced here: 654 us
  waiting for transfers between devices  461 us (69%)
  local copies, waits for them, and re-layouts  76.2 us (11%)
  matrix products  47.1 us (7%)
  other arithmetic  30.8 us (5%)
  starting transfers between devices  24.2 us (4%)
  between operations  14.5 us (2%)
    psum x1, waiting for transfers between devices, body(): lax.psum(jnp.dot(tokens.T, d_logit, preferred_element_type=jnp.float32),...  139 us
    all_gather x1, waiting for transfers between devices, body(): lax.all_gather(w_up, 'dp', axis=1, tiled=True)  67.9 us
    all_gather x1, waiting for transfers between devices, body(): lax.all_gather(w_down, 'dp', axis=1, tiled=True)  67.4 us
    unnamed x33, local copies, waits for them, and re-layouts  57 us
    unnamed x8, waiting for transfers between devices  55.2 us
    all_to_all x1, waiting for transfers between devices, body(): lax.all_to_all(picked, 'expert', split_axis=0, concat_axis=1, tiled=True)  49.5 us
    all_to_all x1, waiting for transfers between devices, body(): lax.all_to_all(expert_out, 'expert', split_axis=1, concat_axis=0, tiled=T...  46.3 us
    unnamed x2, other arithmetic  25.4 us
  transfers between devices with their start and end apart: 10, of which 8 were waited for; matrix products, arithmetic and copies ran while one was open for 20% of the time, Pallas kernels for 0%

commit v1 on v0

--- a/solution.py
+++ b/solution.py
@@ -1,7 +1,114 @@
+import functools
+
 import jax
 import jax.numpy as jnp
 from jax import lax
+from jax.experimental import pallas as pl
+from jax.experimental.pallas import tpu as pltpu
 from jax.sharding import PartitionSpec as P
+
+MESH = pl.DeviceIdType.MESH
+
+
+def _gather_kernel(n, *refs):
+    count = (len(refs) - 3) // 2
+    srcs, dsts = refs[:count], refs[count : 2 * count]
+    send_sem, recv_sem, local_sem = refs[2 * count :]
+    me = lax.axis_index("dp")
+    ex = lax.axis_index("expert")
+    barrier = pltpu.get_barrier_semaphore()
+    for k in range(1, n):
+        pl.semaphore_signal(barrier, inc=1, device_id=(lax.rem(me + k, n), ex), device_id_type=MESH)
+    pl.semaphore_wait(barrier, n - 1)
+    copies = []
+    for a in range(count):
+        rows = srcs[a].shape[0]
+        slot = dsts[a].at[pl.ds(me * rows, rows)]
+        local = pltpu.make_async_copy(srcs[a], slot, local_sem.at[a])
+        local.start()
+        copies.append(local)
+        for k in range(1, n):
+            remote = pltpu.make_async_remote_copy(
+                src_ref=srcs[a],
+                dst_ref=slot,
+                send_sem=send_sem.at[a, k],
+                recv_sem=recv_sem.at[a, k],
+                device_id=(lax.rem(me + k, n), ex),
+                device_id_type=MESH,
+            )
+            remote.start()
+            copies.append(remote)
+    for c in copies:
+        c.wait()
+
+
+def dp_all_gather(shards, n):
+    count = len(shards)
+    return pl.pallas_call(
+        functools.partial(_gather_kernel, n),
+        out_shape=[jax.ShapeDtypeStruct((n * s.shape[0],) + s.shape[1:], s.dtype) for s in shards],
+        in_specs=[pl.BlockSpec(memory_space=pl.ANY)] * count,
+        out_specs=[pl.BlockSpec(memory_space=pl.ANY)] * count,
+        scratch_shapes=[
+            pltpu.SemaphoreType.DMA((count, n)),
+            pltpu.SemaphoreType.DMA((count, n)),
+            pltpu.SemaphoreType.DMA((count,)),
+        ],
+        compiler_params=pltpu.CompilerParams(collective_id=0, has_side_effects=True),
+    )(*shards)
+
+
+def _scatter_kernel(n, *refs):
+    count = (len(refs) - 3) // 2
+    srcs, dsts = refs[:count], refs[count : 2 * count]
+    send_sem, recv_sem, local_sem = refs[2 * count :]
+    me = lax.axis_index("dp")
+    ex = lax.axis_index("expert")
+    barrier = pltpu.get_barrier_semaphore()
+    for k in range(1, n):
+        pl.semaphore_signal(barrier, inc=1, device_id=(lax.rem(me + k, n), ex), device_id_type=MESH)
+    pl.semaphore_wait(barrier, n - 1)
+    copies = []
+    for a in range(count):
+        rows = dsts[a].shape[1]
+        local = pltpu.make_async_copy(
+            srcs[a].at[pl.ds(me * rows, rows)], dsts[a].at[me], local_sem.at[a]
+        )
+        local.start()
+        copies.append(local)
+        for k in range(1, n):
+            peer = lax.rem(me + k, n)
+            remote = pltpu.make_async_remote_copy(
+                src_ref=srcs[a].at[pl.ds(peer * rows, rows)],
+                dst_ref=dsts[a].at[me],
+                send_sem=send_sem.at[a, k],
+                recv_sem=recv_sem.at[a, k],
+                device_id=(peer, ex),
+                device_id_type=MESH,
+            )
+            remote.start()
+            copies.append(remote)
+    for c in copies:
+        c.wait()
+
+
+def dp_reduce_scatter(partials, n):
+    count = len(partials)
+    received = pl.pallas_call(
+        functools.partial(_scatter_kernel, n),
+        out_shape=[
+            jax.ShapeDtypeStruct((n, p.shape[0] // n) + p.shape[1:], p.dtype) for p in partials
+        ],
+        in_specs=[pl.BlockSpec(memory_space=pl.ANY)] * count,
+        out_specs=[pl.BlockSpec(memory_space=pl.ANY)] * count,
+        scratch_shapes=[
+            pltpu.SemaphoreType.DMA((count, n)),
+            pltpu.SemaphoreType.DMA((count, n)),
+            pltpu.SemaphoreType.DMA((count,)),
+        ],
+        compiler_params=pltpu.CompilerParams(collective_id=1, has_side_effects=True),
+    )(*partials)
+    return [jnp.sum(r.astype(jnp.float32), axis=0) for r in received]
 
 
 def to_blocks(slot_array, num_blocks, pick_count):
@@ -14,30 +121,19 @@
     )
 
 
-def weight_grads(expert_rows, hidden, expert_cot, d_pre_gate, d_pre_up):
+def weight_grads(expert_rows, hidden, expert_cot, d_pre_gate, d_pre_up, n):
     hidden_activations = hidden.shape[2]
     both_grads = jnp.concatenate([d_pre_gate, d_pre_up], axis=2)
-    columns = expert_rows
-    in_share = lax.psum_scatter(
-        jnp.einsum("erc,erk->cek", columns, both_grads, preferred_element_type=jnp.float32).astype(
-            jnp.bfloat16
-        ),
-        "dp",
-        scatter_dimension=0,
-        tiled=True,
-    ).astype(jnp.float32)
-    grad_gate = jnp.transpose(in_share[:, :, :hidden_activations], (1, 0, 2))
-    grad_up = jnp.transpose(in_share[:, :, hidden_activations:], (1, 0, 2))
-    columns = hidden
-    out_share = lax.psum_scatter(
-        jnp.einsum("erc,erd->ced", columns, expert_cot, preferred_element_type=jnp.float32).astype(
-            jnp.bfloat16
-        ),
-        "dp",
-        scatter_dimension=0,
-        tiled=True,
-    ).astype(jnp.float32)
-    down_weight_gradient = jnp.transpose(out_share, (1, 0, 2))
+    in_part = jnp.einsum(
+        "erc,erk->ck", expert_rows, both_grads, preferred_element_type=jnp.float32
+    ).astype(jnp.bfloat16)
+    out_part = jnp.einsum(
+        "erc,erd->cd", hidden, expert_cot, preferred_element_type=jnp.float32
+    ).astype(jnp.bfloat16)
+    in_share, out_share = dp_reduce_scatter([in_part, out_part], n)
+    grad_gate = in_share[None, :, :hidden_activations]
+    grad_up = in_share[None, :, hidden_activations:]
+    down_weight_gradient = out_share[None]
     return (grad_gate, grad_up, down_weight_gradient)
 
 
@@ -54,10 +150,9 @@
     slot_gate_values = jnp.take_along_axis(gate_values.T, slot_rows, axis=1)
     cot_rows = cotangent[slot_rows]
     scaled_cot = (slot_gate_values[:, :, None] * cot_rows.astype(jnp.float32)).astype(jnp.bfloat16)
+    n = lax.axis_size("dp")
     full_gate, full_up, full_down = (
-        lax.all_gather(w_gate, "dp", axis=1, tiled=True),
-        lax.all_gather(w_up, "dp", axis=1, tiled=True),
-        lax.all_gather(w_down, "dp", axis=1, tiled=True),
+        g[None] for g in dp_all_gather([w_gate[0], w_up[0], w_down[0]], n)
     )
     expert_rows = lax.all_to_all(picked, "expert", split_axis=0, concat_axis=1, tiled=True)
     pre_gate = jnp.einsum(
@@ -119,7 +214,7 @@
         jnp.dot(tokens.T, d_logit, preferred_element_type=jnp.float32), ("dp", "expert")
     )
     grad_gate, grad_up, down_weight_gradient = weight_grads(
-        expert_rows, hidden, expert_cot, d_pre_gate, d_pre_up
+        expert_rows, hidden, expert_cot, d_pre_gate, d_pre_up, n
     )
     return (mixed, grad_tokens, grad_gate, grad_up, down_weight_gradient, grad_router)
 

time: 665 us -> 628 us (0.944)
  waiting for transfers between devices: 461 us -> 154 us
  Pallas kernels: 0 us -> 283 us
  local copies, waits for them, and re-layouts: 76.2 us -> 57.8 us
  other arithmetic: 30.8 us -> 37.8 us
    pallas_call x0 -> x2, Pallas kernels: none -> 283 us  [the longest x1 155 us: dp_reduce_scatter(): pl.pallas_call(functools.partial(_scatter_kernel, n), out_shape=[jax.Shap...]
    all_gather x3 -> x0, waiting for transfers between devices: 158 us -> none  [the longest x1 67.9 us: body(): lax.all_gather(w_up, 'dp', axis=1, tiled=True)]
    unnamed x8 -> x1, waiting for transfers between devices: 55.2 us -> 0.02 us
    all_to_all x1, waiting for transfers between devices: 46.3 us -> 0.01 us  [body(): lax.all_to_all(expert_out, 'expert', split_axis=1, concat_axis=0, tiled=T...]
    all_to_all x1, waiting for transfers between devices: 49.5 us -> 14 us  [body(): lax.all_to_all(picked, 'expert', split_axis=0, concat_axis=1, tiled=True)]
    unnamed x33 -> x36, local copies, waits for them, and re-layouts: 57 us -> 37.6 us
    all_to_all x1, waiting for transfers between devices: 13.2 us -> 0.97 us  [body(): lax.all_to_all(d_rows, 'expert', split_axis=1, concat_axis=0, tiled=True)]
  transfers between devices with their start and end apart: 10 -> 5, of which waited for: 8 -> 3; matrix products, arithmetic and copies ran while one was open for 20% -> 14% of each run, Pallas kernels for 0% -> 45%
where the time goes in v1:
time: 628 us; the launch traced here: 622 us
  Pallas kernels  283 us (45%)
  waiting for transfers between devices  154 us (25%)
  local copies, waits for them, and re-layouts  57.8 us (9%)
  matrix products  45.3 us (7%)
  other arithmetic  37.8 us (6%)
  starting transfers between devices  30 us (5%)
  between operations  14.8 us (2%)
    pallas_call x1, Pallas kernels, dp_reduce_scatter(): pl.pallas_call(functools.partial(_scatter_kernel, n), out_shape=[jax.Shap...  155 us
    psum x1, waiting for transfers between devices, body(): lax.psum(jnp.dot(tokens.T, d_logit, preferred_element_type=jnp.float32),...  139 us
    pallas_call x1, Pallas kernels, dp_all_gather(): pl.pallas_call(functools.partial(_gather_kernel, n), out_shape=[jax.Shape...  128 us
    unnamed x36, local copies, waits for them, and re-layouts  37.6 us
    unnamed x2, other arithmetic  25.2 us
    all_to_all x1, waiting for transfers between devices, body(): lax.all_to_all(picked, 'expert', split_axis=0, concat_axis=1, tiled=True)  14 us
  transfers between devices with their start and end apart: 5, of which 3 were waited for; matrix products, arithmetic and copies ran while one was open for 14% of the time, Pallas kernels for 45%

profile of v1, /device:TPU:5, one launch (start us, length us, event | category | flops | bytes accessed | tf_op | source)
XLA Modules:
  0.0 622.2 jit_solution(4906117859807343256)
XLA Ops:
  8.3 3.0 gather_fusion
  11.3 8.8 %all-to-all-start = ((bf16[16,32,1536]{2,1,0:T(8,128)(2,1)}), bf16[16,32,1536]{2,1,0:T(8,128)(2,1)}, u32[]{:S(2)}, u32[]{:S(2)}) async-start(bf16[16,32,1536]{2,1,0:T(8,128)(2,1)} %bitcast.5), calls=%async_computation | async-start | bytes 3145728 | tf_op jit(solution)/shard_map/all_to_all | solution.py:157
  20.5 4.5 gather_fusion.2
  25.4 2.1 gather_fusion.1
  29.0 14.0 %all-to-all-done = bf16[16,32,1536]{2,1,0:T(8,128)(2,1)} async-done(((bf16[16,32,1536]{2,1,0:T(8,128)(2,1)}), bf16[16,32,1536]{2,1,0:T(8,128)(2,1)}, u32[]{:S(2)}, u32[]{:S(2)}) %all-to-all-start) | async-done | bytes 1572896 | tf_op jit(solution)/shard_map/all_to_all | solution.py:157
  43.0 5.6 all-to-all-start.2
  49.2 127.9 %shard_map.118 = (bf16[1536,1024]{1,0:T(8,128)(2,1)}, bf16[1536,1024]{1,0:T(8,128)(2,1)}, bf16[1024,1536]{1,0:T(8,128)(2,1)}) custom-call(bf16[192,1024]{1,0:T(8,128)(2,1)} %bitcast.112, bf16[192,1024]{1,0:T(8,128)(2,1)} %bitcast.113, bf16[128,1536]{1,0:T(8,128)(2,1)} %bitcast.114), custom_call_target="tpu_custom_call" | custom-call | tf_op jit(solution)/shard_map/pallas_call | solution.py:47
  177.1 5.6 fusion.24
  182.7 4.7 fusion.25
  187.5 7.6 %multiply_convert_fusion.1 = (bf16[512,1024]{1,0:T(8,128)(2,1)}, bf16[512,1024]{1,0:T(8,128)(2,1)}, bf16[512,1024]{1,0:T(8,128)(2,1)S(1)}) fusion(f32[512,1024]{1,0:T(8,128)} %fusion.24, f32[512,1024]{1,0:T(8,128)} %fusion.25, bf16[512,1536]{1,0:T(8,128)(2,1)} %bitcast.18, bf16[1024,1536]{1,0:T(8,128)(2,1)} %get-tuple-element.13), kind=kOutput, calls=%fused_computation.25 | convolution fusion | flops 1618477056 | bytes 12058624 | tf_op jit(solution)/shard_map/erd,ehd->erh/dot_general | solution.py:170
  197.9 4.1 copy.101
  202.5 12.6 %reduce.1 = bf16[512,1536]{1,0:T(8,128)(2,1)} reduce(bf16[512,1,1536]{2,1,0:T(2,128)(2,1)} %bitcast.105, bf16[]{:T(256)} %broadcast.103), dimensions={1}, to_apply=%bitcast.99.reduce_sub_computation | reduce | bytes 3145730
  215.1 5.0 reshape.234
  220.0 8.2 %all-to-all-start.1 = ((bf16[16,2,24576]{2,1,0:T(2,128)(2,1)}), bf16[16,2,24576]{2,1,0:T(2,128)(2,1)}, u32[]{:S(2)}, u32[]{:S(2)}) async-start(bf16[16,2,24576]{2,1,0:T(2,128)(2,1)} %reshape.234), calls=%async_computation.1 | async-start | bytes 3145728 | tf_op jit(solution)/shard_map/all_to_all | solution.py:167
  228.2 4.2 fusion.26
  232.4 1.8 fusion.5
  234.3 4.1 copy.100
  238.3 12.6 %reduce.2 = bf16[512,1536]{1,0:T(8,128)(2,1)} reduce(bf16[512,1,1536]{2,1,0:T(2,128)(2,1)} %bitcast.106, bf16[]{:T(256)} %broadcast.103), dimensions={1}, to_apply=%bitcast.98.reduce_sub_computation | reduce | bytes 3145730
  250.9 5.0 reshape.236
  255.9 5.3 convolution_convert_fusion.1.refs_1_
  261.3 7.0 %convolution_convert_fusion.refs_0_ = bf16[1536,2048]{1,0:T(8,128)(2,1)} fusion(bf16[512,1536]{1,0:T(8,128)(2,1)} %bitcast.6, bf16[1,512,1024]{2,1,0:T(8,128)(2,1)S(1)} %bitcast.116, bf16[1,512,1024]{2,1,0:T(8,128)(2,1)S(1)} %bitcast.117), kind=kOutput, calls=%fused_computation.4 | convolution fusion | flops 3228565504 | bytes 9961472 | tf_op jit(solution)/shard_map/erc,erk->ck/dot_general | solution.py:127
  268.2 154.9 %shard_map.119 = (bf16[8,192,2048]{2,1,0:T(8,128)(2,1)}, bf16[8,128,1536]{2,1,0:T(8,128)(2,1)}) custom-call(bf16[1536,2048]{1,0:T(8,128)(2,1)} %convolution_convert_fusion.refs_0_, bf16[1024,1536]{1,0:T(8,128)(2,1)} %convolution_convert_fusion.1.refs_1_), custom_call_target="tpu_custom_call" | custom-call | tf_op jit(solution)/shard_map/pallas_call | solution.py:97
  423.2 7.5 %all-to-all-start.3 = ((bf16[16,2,24576]{2,1,0:T(2,128)(2,1)}), bf16[16,2,24576]{2,1,0:T(2,128)(2,1)}, u32[]{:S(2)}, u32[]{:S(2)}) async-start(bf16[16,2,24576]{2,1,0:T(2,128)(2,1)} %reshape.236), calls=%async_computation.3 | async-start | bytes 3145728 | tf_op jit(solution)/shard_map/all_to_all | solution.py:180
  430.7 4.3 convert_reduce_fusion
  437.6 10.3 %reshape.235 = bf16[512,1,1536]{2,1,0:T(2,128)(2,1)} reshape(bf16[16,2,24576]{2,1,0:T(2,128)(2,1)} %all-to-all-done.1) | data formatting | bytes 3145728
  447.9 2.5 fusion
  450.8 1.9 copy_convert_fusion
  453.6 10.1 %reshape.237 = bf16[512,1,1536]{2,1,0:T(2,128)(2,1)} reshape(bf16[16,2,24576]{2,1,0:T(2,128)(2,1)} %all-to-all-done.3) | data formatting | bytes 3145728
  463.7 3.4 copy.80
  468.6 1.9 fusion.11
  470.9 2.4 fusion.6
  474.6 138.7 %all-reduce.2.cloned.1.call-done = f32[1536,16]{0,1:T(8,128)} async-done(((f32[1536,16]{0,1:T(8,128)}), f32[1536,16]{0,1:T(8,128)}) %all-reduce.2.cloned.1.call-update) | async-done | bytes 98320 | tf_op jit(solution)/shard_map/psum | solution.py:213
  (65 shorter events, 15.9 us)
Async XLA Ops:
  7.2 1.2 copy-start
  11.3 8.9 %copy-start.6 = (bf16[1536,16]{0,1:T(8,128)(2,1)S(1)}, bf16[1536,16]{0,1:T(8,128)(2,1)}, u32[]{:S(2)}) copy-start(bf16[1536,16]{0,1:T(8,128)(2,1)} %param.10) | copy-start | bytes 147460
  11.3 31.7 %all-to-all-start = ((bf16[16,32,1536]{2,1,0:T(8,128)(2,1)}), bf16[16,32,1536]{2,1,0:T(8,128)(2,1)}, u32[]{:S(2)}, u32[]{:S(2)}) async-start(bf16[16,32,1536]{2,1,0:T(8,128)(2,1)} %bitcast.5), calls=%async_computation | async-start | bytes 3145728 | tf_op jit(solution)/shard_map/all_to_all | solution.py:157
  20.5 4.7 copy-start.5
  20.5 4.8 copy-start.1
  43.0 144.5 %all-to-all-start.2 = ((bf16[16,32,1536]{2,1,0:T(8,128)(2,1)}), bf16[16,32,1536]{2,1,0:T(8,128)(2,1)}, u32[]{:S(2)}, u32[]{:S(2)}) async-start(bf16[16,32,1536]{2,1,0:T(8,128)(2,1)} %multiply_convert_fusion), calls=%async_computation.2 | async-start | bytes 3145728 | tf_op jit(solution)/shard_map/all_to_all | solution.py:168
  177.1 5.6 copy-start.7
  187.5 8.6 %copy-start.9 = (bf16[1024,1536]{1,0:T(8,128)(2,1)S(1)}, bf16[1024,1536]{1,0:T(8,128)(2,1)}, u32[]{:S(2)}) copy-start(bf16[1024,1536]{1,0:T(8,128)(2,1)} %get-tuple-element.13) | copy-start | bytes 9437188
  195.1 1.0 copy-start.13
  220.0 203.1 %all-to-all-start.1 = ((bf16[16,2,24576]{2,1,0:T(2,128)(2,1)}), bf16[16,2,24576]{2,1,0:T(2,128)(2,1)}, u32[]{:S(2)}, u32[]{:S(2)}) async-start(bf16[16,2,24576]{2,1,0:T(2,128)(2,1)} %reshape.234), calls=%async_computation.1 | async-start | bytes 3145728 | tf_op jit(solution)/shard_map/all_to_all | solution.py:167
  228.2 4.2 copy-start.8
  228.2 4.2 copy-start.10
  255.9 5.4 copy-start.11
  255.9 5.4 copy-start.12
  423.2 30.4 %all-to-all-start.3 = ((bf16[16,2,24576]{2,1,0:T(2,128)(2,1)}), bf16[16,2,24576]{2,1,0:T(2,128)(2,1)}, u32[]{:S(2)}, u32[]{:S(2)}) async-start(bf16[16,2,24576]{2,1,0:T(2,128)(2,1)} %reshape.236), calls=%async_computation.3 | async-start | bytes 3145728 | tf_op jit(solution)/shard_map/all_to_all | solution.py:180
  430.6 182.7 %all-reduce.2.cloned.1.call-start = ((), (), s32[]{:S(2)}) async-start(), calls=%async_computation.4 | async-start | bytes 196608 | tf_op jit(solution)/shard_map/psum | solution.py:213
  430.7 4.3 copy-start.4
  447.9 2.8 copy-start.2
  468.6 2.4 copy-start.3
Sparse Core Ops, SparseCore 0:
  468.7 144.6 all-reduce.1

commit v2 on v1

--- a/solution.py
+++ b/solution.py
@@ -58,7 +58,7 @@
     )(*shards)
 
 
-def _scatter_kernel(n, *refs):
+def _exchange_kernel(n, n_scatter, *refs):
     count = (len(refs) - 3) // 2
     srcs, dsts = refs[:count], refs[count : 2 * count]
     send_sem, recv_sem, local_sem = refs[2 * count :]
@@ -71,15 +71,21 @@
     copies = []
     for a in range(count):
         rows = dsts[a].shape[1]
-        local = pltpu.make_async_copy(
-            srcs[a].at[pl.ds(me * rows, rows)], dsts[a].at[me], local_sem.at[a]
-        )
+        if a < n_scatter:
+            mine = srcs[a].at[pl.ds(me * rows, rows)]
+        else:
+            mine = srcs[a]
+        local = pltpu.make_async_copy(mine, dsts[a].at[me], local_sem.at[a])
         local.start()
         copies.append(local)
         for k in range(1, n):
             peer = lax.rem(me + k, n)
+            if a < n_scatter:
+                part = srcs[a].at[pl.ds(peer * rows, rows)]
+            else:
+                part = srcs[a]
             remote = pltpu.make_async_remote_copy(
-                src_ref=srcs[a].at[pl.ds(peer * rows, rows)],
+                src_ref=part,
                 dst_ref=dsts[a].at[me],
                 send_sem=send_sem.at[a, k],
                 recv_sem=recv_sem.at[a, k],
@@ -92,13 +98,14 @@
         c.wait()
 
 
-def dp_reduce_scatter(partials, n):
-    count = len(partials)
+def dp_exchange(partials, replicas, n):
+    arrays = list(partials) + list(replicas)
+    count = len(arrays)
+    shapes = [(n, p.shape[0] // n) + p.shape[1:] for p in partials]
+    shapes += [(n,) + r.shape for r in replicas]
     received = pl.pallas_call(
-        functools.partial(_scatter_kernel, n),
-        out_shape=[
-            jax.ShapeDtypeStruct((n, p.shape[0] // n) + p.shape[1:], p.dtype) for p in partials
-        ],
+        functools.partial(_exchange_kernel, n, len(partials)),
+        out_shape=[jax.ShapeDtypeStruct(s, a.dtype) for s, a in zip(shapes, arrays)],
         in_specs=[pl.BlockSpec(memory_space=pl.ANY)] * count,
         out_specs=[pl.BlockSpec(memory_space=pl.ANY)] * count,
         scratch_shapes=[
@@ -107,7 +114,7 @@
             pltpu.SemaphoreType.DMA((count,)),
         ],
         compiler_params=pltpu.CompilerParams(collective_id=1, has_side_effects=True),
-    )(*partials)
+    )(*arrays)
     return [jnp.sum(r.astype(jnp.float32), axis=0) for r in received]
 
 
@@ -121,7 +128,7 @@
     )
 
 
-def weight_grads(expert_rows, hidden, expert_cot, d_pre_gate, d_pre_up, n):
+def weight_grads(expert_rows, hidden, expert_cot, d_pre_gate, d_pre_up, router_part, n):
     hidden_activations = hidden.shape[2]
     both_grads = jnp.concatenate([d_pre_gate, d_pre_up], axis=2)
     in_part = jnp.einsum(
@@ -130,11 +137,11 @@
     out_part = jnp.einsum(
         "erc,erd->cd", hidden, expert_cot, preferred_element_type=jnp.float32
     ).astype(jnp.bfloat16)
-    in_share, out_share = dp_reduce_scatter([in_part, out_part], n)
+    in_share, out_share, grad_router = dp_exchange([in_part, out_part], [router_part], n)
     grad_gate = in_share[None, :, :hidden_activations]
     grad_up = in_share[None, :, hidden_activations:]
     down_weight_gradient = out_share[None]
-    return (grad_gate, grad_up, down_weight_gradient)
+    return (grad_gate, grad_up, down_weight_gradient, grad_router)
 
 
 def body(tokens, cotangent, chosen, w_router, w_gate, w_up, w_down):
@@ -210,11 +217,11 @@
     grad_tokens = (
         gathered_grads + jnp.dot(d_logit, w_router.T, preferred_element_type=jnp.float32)
     ).astype(jnp.bfloat16)
-    grad_router = lax.psum(
-        jnp.dot(tokens.T, d_logit, preferred_element_type=jnp.float32), ("dp", "expert")
-    )
-    grad_gate, grad_up, down_weight_gradient = weight_grads(
-        expert_rows, hidden, expert_cot, d_pre_gate, d_pre_up, n
+    router_part = lax.psum(
+        jnp.dot(tokens.T, d_logit, preferred_element_type=jnp.float32), "expert"
+    )
+    grad_gate, grad_up, down_weight_gradient, grad_router = weight_grads(
+        expert_rows, hidden, expert_cot, d_pre_gate, d_pre_up, router_part, n
     )
     return (mixed, grad_tokens, grad_gate, grad_up, down_weight_gradient, grad_router)
 

time: 628 us -> 732 us (1.17)
  the two profiles are of different devices: /device:TPU:5 before, /device:TPU:76 now
where the time goes in v2:
time: 732 us; the launch traced here: 727 us
  Pallas kernels  399 us (55%)
  waiting for transfers between devices  141 us (19%)
  local copies, waits for them, and re-layouts  58.3 us (8%)
  matrix products  45.2 us (6%)
  other arithmetic  41 us (6%)
  starting transfers between devices  28 us (4%)
  between operations  14.8 us (2%)
    pallas_call x1, Pallas kernels, dp_exchange(): pl.pallas_call(functools.partial(_exchange_kernel, n, len(partials)), out...  262 us
    pallas_call x1, Pallas kernels, dp_all_gather(): pl.pallas_call(functools.partial(_gather_kernel, n), out_shape=[jax.Shape...  137 us
    psum x1, waiting for transfers between devices, body(): lax.psum(jnp.dot(tokens.T, d_logit, preferred_element_type=jnp.float32),...  128 us
    unnamed x32, local copies, waits for them, and re-layouts  38.1 us
    unnamed x2, other arithmetic  25.2 us
  transfers between devices with their start and end apart: 5, of which 2 were waited for; matrix products, arithmetic and copies ran while one was open for 11% of the time, Pallas kernels for 19%

profile of v2, /device:TPU:76, one launch (start us, length us, event | category | flops | bytes accessed | tf_op | source)
XLA Modules:
  0.0 727.2 jit_solution(14209777979909519792)
XLA Ops:
  8.3 2.9 gather_fusion
  11.3 6.8 all-to-all-start
  18.6 4.5 gather_fusion.2
  23.5 2.1 gather_fusion.1
  27.1 12.6 %all-to-all-done = bf16[16,32,1536]{2,1,0:T(8,128)(2,1)} async-done(((bf16[16,32,1536]{2,1,0:T(8,128)(2,1)}), bf16[16,32,1536]{2,1,0:T(8,128)(2,1)}, u32[]{:S(2)}, u32[]{:S(2)}) %all-to-all-start) | async-done | bytes 1572896 | tf_op jit(solution)/shard_map/all_to_all | solution.py:164
  39.7 7.1 all-to-all-start.2
  47.4 137.3 %shard_map.118 = (bf16[1536,1024]{1,0:T(8,128)(2,1)}, bf16[1536,1024]{1,0:T(8,128)(2,1)}, bf16[1024,1536]{1,0:T(8,128)(2,1)}) custom-call(bf16[192,1024]{1,0:T(8,128)(2,1)} %bitcast.112, bf16[192,1024]{1,0:T(8,128)(2,1)} %bitcast.113, bf16[128,1536]{1,0:T(8,128)(2,1)} %bitcast.114), custom_call_target="tpu_custom_call" | custom-call | tf_op jit(solution)/shard_map/pallas_call | solution.py:47
  184.7 5.6 fusion.24
  190.3 4.7 fusion.25
  195.0 7.6 %multiply_convert_fusion.1 = (bf16[512,1024]{1,0:T(8,128)(2,1)}, bf16[512,1024]{1,0:T(8,128)(2,1)}, bf16[512,1024]{1,0:T(8,128)(2,1)S(1)}) fusion(f32[512,1024]{1,0:T(8,128)} %fusion.24, f32[512,1024]{1,0:T(8,128)} %fusion.25, bf16[512,1536]{1,0:T(8,128)(2,1)} %bitcast.18, bf16[1024,1536]{1,0:T(8,128)(2,1)} %get-tuple-element.14), kind=kOutput, calls=%fused_computation.25 | convolution fusion | flops 1618477056 | bytes 12058624 | tf_op jit(solution)/shard_map/erd,ehd->erh/dot_general | solution.py:177
  205.4 4.1 copy.111
  210.0 12.6 %reduce.1 = bf16[512,1536]{1,0:T(8,128)(2,1)} reduce(bf16[512,1,1536]{2,1,0:T(2,128)(2,1)} %bitcast.105, bf16[]{:T(256)} %broadcast.103), dimensions={1}, to_apply=%bitcast.99.reduce_sub_computation | reduce | bytes 3145730
  222.6 5.0 reshape.234
  227.6 6.8 all-to-all-start.1
  234.4 4.2 fusion.26
  238.6 1.8 fusion.5
  240.5 4.1 copy.110
  244.5 12.6 %reduce.2 = bf16[512,1536]{1,0:T(8,128)(2,1)} reduce(bf16[512,1,1536]{2,1,0:T(2,128)(2,1)} %bitcast.106, bf16[]{:T(256)} %broadcast.103), dimensions={1}, to_apply=%bitcast.98.reduce_sub_computation | reduce | bytes 3145730
  257.2 5.0 reshape.236
  262.1 5.2 convolution_convert_fusion.1.refs_1_
  267.4 7.2 all-to-all-start.3
  274.6 8.1 %convolution_convert_fusion.refs_0_ = bf16[1536,2048]{1,0:T(8,128)(2,1)} fusion(bf16[512,1536]{1,0:T(8,128)(2,1)} %bitcast.6, bf16[1,512,1024]{2,1,0:T(8,128)(2,1)} %bitcast.116, bf16[1,512,1024]{2,1,0:T(8,128)(2,1)} %bitcast.117), kind=kOutput, calls=%fused_computation.4 | convolution fusion | flops 3228565504 | bytes 9961472 | tf_op jit(solution)/shard_map/erc,erk->ck/dot_general | solution.py:134
  282.8 10.3 %reshape.235 = bf16[512,1,1536]{2,1,0:T(2,128)(2,1)} reshape(bf16[16,2,24576]{2,1,0:T(2,128)(2,1)} %all-to-all-done.1) | data formatting | bytes 3145728
  293.1 2.5 fusion
  295.9 1.9 copy_convert_fusion
  297.8 10.0 %reshape.237 = bf16[512,1,1536]{2,1,0:T(2,128)(2,1)} reshape(bf16[16,2,24576]{2,1,0:T(2,128)(2,1)} %all-to-all-done.3) | data formatting | bytes 3145728
  307.8 2.2 copy.90
  313.9 2.4 fusion.6
  317.6 128.3 %all-reduce.2.cloned.1.call-done.refs_2_ = f32[1536,16]{1,0:T(8,128)} async-done(((f32[1536,16]{1,0:T(8,128)}), f32[1536,16]{1,0:T(8,128)}) %all-reduce.2.cloned.1.call-update) | async-done | bytes 98320 | tf_op jit(solution)/shard_map/psum | solution.py:220
  445.9 261.8 %shard_map.119 = (bf16[8,192,2048]{2,1,0:T(8,128)(2,1)}, bf16[8,128,1536]{2,1,0:T(8,128)(2,1)}, f32[8,1536,16]{2,1,0:T(8,128)}) custom-call(bf16[1536,2048]{1,0:T(8,128)(2,1)} %convolution_convert_fusion.refs_0_, bf16[1024,1536]{1,0:T(8,128)(2,1)} %convolution_convert_fusion.1.refs_1_, f32[1536,16]{1,0:T(8,128)} %all-reduce.2.cloned.1.call-done.refs_2_), custom_call_target="tpu_custom_call" | custom-call | tf_op jit(solution)/shard_map/pallas_call | solution.py:106
  707.7 4.2 convert_reduce_fusion
  715.7 3.3 reduce_sum.39
  (62 shorter events, 17.5 us)
Async XLA Ops:
  7.2 1.2 copy-start
  11.3 7.0 copy-start.6
  11.3 28.4 %all-to-all-start = ((bf16[16,32,1536]{2,1,0:T(8,128)(2,1)}), bf16[16,32,1536]{2,1,0:T(8,128)(2,1)}, u32[]{:S(2)}, u32[]{:S(2)}) async-start(bf16[16,32,1536]{2,1,0:T(8,128)(2,1)} %bitcast.5), calls=%async_computation | async-start | bytes 3145728 | tf_op jit(solution)/shard_map/all_to_all | solution.py:164
  18.6 4.7 copy-start.5
  18.6 4.8 copy-start.1
  39.7 155.3 %all-to-all-start.2 = ((bf16[16,32,1536]{2,1,0:T(8,128)(2,1)}), bf16[16,32,1536]{2,1,0:T(8,128)(2,1)}, u32[]{:S(2)}, u32[]{:S(2)}) async-start(bf16[16,32,1536]{2,1,0:T(8,128)(2,1)} %multiply_convert_fusion), calls=%async_computation.2 | async-start | bytes 3145728 | tf_op jit(solution)/shard_map/all_to_all | solution.py:175
  184.7 5.6 copy-start.7
  195.0 8.6 %copy-start.9 = (bf16[1024,1536]{1,0:T(8,128)(2,1)S(1)}, bf16[1024,1536]{1,0:T(8,128)(2,1)}, u32[]{:S(2)}) copy-start(bf16[1024,1536]{1,0:T(8,128)(2,1)} %get-tuple-element.14) | copy-start | bytes 9437188
  202.6 1.0 copy-start.11
  227.6 39.8 %all-to-all-start.1 = ((bf16[16,2,24576]{2,1,0:T(2,128)(2,1)}), bf16[16,2,24576]{2,1,0:T(2,128)(2,1)}, u32[]{:S(2)}, u32[]{:S(2)}) async-start(bf16[16,2,24576]{2,1,0:T(2,128)(2,1)} %reshape.234), calls=%async_computation.1 | async-start | bytes 3145728 | tf_op jit(solution)/shard_map/all_to_all | solution.py:174
  234.4 4.2 copy-start.8
  234.4 4.2 copy-start.10
  267.4 30.5 %all-to-all-start.3 = ((bf16[16,2,24576]{2,1,0:T(2,128)(2,1)}), bf16[16,2,24576]{2,1,0:T(2,128)(2,1)}, u32[]{:S(2)}, u32[]{:S(2)}) async-start(bf16[16,2,24576]{2,1,0:T(2,128)(2,1)} %reshape.236), calls=%async_computation.3 | async-start | bytes 3145728 | tf_op jit(solution)/shard_map/all_to_all | solution.py:187
  274.6 171.3 %all-reduce.2.cloned.1.call-start = ((), (), s32[]{:S(2)}) async-start(), calls=%async_computation.4 | async-start | bytes 1572864 | tf_op jit(solution)/shard_map/psum | solution.py:220
  293.1 2.8 copy-start.2
  312.0 1.9 copy-start.3
  711.9 2.5 copy-start.4
Sparse Core Ops, SparseCore 0:
  312.1 133.7 all-reduce.1

commit v3 on v2

--- a/solution.py
+++ b/solution.py
@@ -161,7 +161,8 @@
     full_gate, full_up, full_down = (
         g[None] for g in dp_all_gather([w_gate[0], w_up[0], w_down[0]], n)
     )
-    expert_rows = lax.all_to_all(picked, "expert", split_axis=0, concat_axis=1, tiled=True)
+    expert_count_axis = lax.axis_size("expert")
+    expert_rows = lax.all_to_all(picked, "expert", 0, 0, tiled=True).reshape(1, -1, model_width)
     pre_gate = jnp.einsum(
         "erd,edh->erh", expert_rows, full_gate, preferred_element_type=jnp.float32
     )
@@ -171,8 +172,10 @@
     expert_out = jnp.einsum(
         "erh,ehd->erd", hidden, full_down, preferred_element_type=jnp.float32
     ).astype(jnp.bfloat16)
-    returned = lax.all_to_all(expert_out, "expert", split_axis=1, concat_axis=0, tiled=True)
-    expert_cot = lax.all_to_all(scaled_cot, "expert", split_axis=0, concat_axis=1, tiled=True)
+    returned = lax.all_to_all(
+        expert_out.reshape(expert_count_axis, -1, model_width), "expert", 0, 0, tiled=True
+    )
+    expert_cot = lax.all_to_all(scaled_cot, "expert", 0, 0, tiled=True).reshape(1, -1, model_width)
     back_gate, back_up, back_down = (full_gate, full_up, full_down)
     d_hidden = jnp.einsum("erd,ehd->erh", expert_cot, back_down, preferred_element_type=jnp.float32)
     gate_sigmoid = jax.nn.sigmoid(pre_gate)
@@ -184,7 +187,9 @@
         jnp.einsum("erh,edh->erd", d_pre_gate, back_gate, preferred_element_type=jnp.float32)
         + jnp.einsum("erh,edh->erd", d_pre_up, back_up, preferred_element_type=jnp.float32)
     ).astype(jnp.bfloat16)
-    row_grads = lax.all_to_all(d_rows, "expert", split_axis=1, concat_axis=0, tiled=True)
+    row_grads = lax.all_to_all(
+        d_rows.reshape(expert_count_axis, -1, model_width), "expert", 0, 0, tiled=True
+    )
     position_hits = chosen[:, :, :, None] == jnp.arange(block_rows, dtype=jnp.int32)
     indicator_matrix = position_hits.reshape(num_blocks, expert_count * pick_count, block_rows)
     gate_weighted_rows = to_blocks(slot_gate_values, num_blocks, pick_count)[
@@ -217,12 +222,21 @@
     grad_tokens = (
         gathered_grads + jnp.dot(d_logit, w_router.T, preferred_element_type=jnp.float32)
     ).astype(jnp.bfloat16)
-    router_part = lax.psum(
-        jnp.dot(tokens.T, d_logit, preferred_element_type=jnp.float32), "expert"
+    router_full = jnp.dot(tokens.T, d_logit, preferred_element_type=jnp.float32)
+    router_part = jnp.sum(
+        lax.all_to_all(router_full.reshape(expert_count_axis, -1, 128), "expert", 0, 0, tiled=True),
+        axis=0,
     )
     grad_gate, grad_up, down_weight_gradient, grad_router = weight_grads(
         expert_rows, hidden, expert_cot, d_pre_gate, d_pre_up, router_part, n
     )
+    grad_router = lax.all_to_all(
+        jnp.broadcast_to(grad_router[None], (expert_count_axis,) + grad_router.shape),
+        "expert",
+        0,
+        0,
+        tiled=True,
+    ).reshape(router_full.shape)
     return (mixed, grad_tokens, grad_gate, grad_up, down_weight_gradient, grad_router)
 
 

time: 732 us -> 450 us (0.61)
  the two profiles are of different devices: /device:TPU:76 before, /device:TPU:5 now
where the time goes in v3:
time: 450 us; the launch traced here: 449 us
  Pallas kernels  289 us (64%)
  waiting for transfers between devices  47.2 us (10%)
  matrix products  46.5 us (10%)
  starting transfers between devices  37.4 us (8%)
  local copies, waits for them, and re-layouts  15.3 us (3%)
  other arithmetic  12.5 us (3%)
    pallas_call x1, Pallas kernels, dp_exchange(): pl.pallas_call(functools.partial(_exchange_kernel, n, len(partials)), out...  161 us
    pallas_call x1, Pallas kernels, dp_all_gather(): pl.pallas_call(functools.partial(_gather_kernel, n), out_shape=[jax.Shape...  128 us
    all_to_all x1, waiting for transfers between devices, body(): lax.all_to_all(picked, 'expert', 0, 0, tiled=True)  14 us
    all_to_all x1, waiting for transfers between devices, body(): lax.all_to_all(expert_out.reshape(expert_count_axis, -1, model_width), 'e...  12.7 us
    all_to_all x1, waiting for transfers between devices, body(): lax.all_to_all(d_rows.reshape(expert_count_axis, -1, model_width), 'exper...  12.4 us
  transfers between devices with their start and end apart: 6, of which 5 were waited for; matrix products, arithmetic and copies ran while one was open for 11% of the time, Pallas kernels for 29%

profile of v3, /device:TPU:5, one launch (start us, length us, event | category | flops | bytes accessed | tf_op | source)
XLA Modules:
  0.0 448.7 jit_solution(7238606013006321243)
XLA Ops:
  1.8 3.0 gather_fusion
  4.8 8.8 %all-to-all-start = ((bf16[16,32,1536]{2,1,0:T(8,128)(2,1)}), bf16[16,32,1536]{2,1,0:T(8,128)(2,1)}, u32[]{:S(2)}, u32[]{:S(2)}) async-start(bf16[16,32,1536]{2,1,0:T(8,128)(2,1)} %bitcast.5), calls=%async_computation | async-start | bytes 3145728 | tf_op jit(solution)/shard_map/all_to_all | solution.py:165
  14.0 4.5 %gather_fusion.2 = f32[512]{0:T(512)S(1)} fusion(f32[16,256]{1,0:T(8,128)S(1)} %bitcast.97, s32[512]{0:T(512)S(1)} %reshape.211), kind=kCustom, calls=%fused_computation.2 | custom fusion | bytes 8192 | tf_op jit(solution)/shard_map/jit(take_along_axis)/gather | solution.py:157
  18.9 2.1 gather_fusion.1
  21.0 1.5 fusion
  22.5 14.0 %all-to-all-done = bf16[16,32,1536]{2,1,0:T(8,128)(2,1)} async-done(((bf16[16,32,1536]{2,1,0:T(8,128)(2,1)}), bf16[16,32,1536]{2,1,0:T(8,128)(2,1)}, u32[]{:S(2)}, u32[]{:S(2)}) %all-to-all-start) | async-done | bytes 1572896 | tf_op jit(solution)/shard_map/all_to_all | solution.py:165
  36.5 5.1 %all-to-all-start.2 = ((bf16[16,32,1536]{2,1,0:T(8,128)(2,1)}), bf16[16,32,1536]{2,1,0:T(8,128)(2,1)}, u32[]{:S(2)}, u32[]{:S(2)}) async-start(bf16[16,32,1536]{2,1,0:T(8,128)(2,1)} %fusion), calls=%async_computation.2 | async-start | bytes 3145728 | tf_op jit(solution)/shard_map/all_to_all | solution.py:178
  42.1 128.0 %shard_map.118 = (bf16[1536,1024]{1,0:T(8,128)(2,1)}, bf16[1536,1024]{1,0:T(8,128)(2,1)}, bf16[1024,1536]{1,0:T(8,128)(2,1)}) custom-call(bf16[192,1024]{1,0:T(8,128)(2,1)} %bitcast.103, bf16[192,1024]{1,0:T(8,128)(2,1)} %bitcast.104, bf16[128,1536]{1,0:T(8,128)(2,1)} %bitcast.105), custom_call_target="tpu_custom_call" | custom-call | tf_op jit(solution)/shard_map/pallas_call | solution.py:47
  170.1 5.6 %fusion.22 = f32[512,1024]{1,0:T(8,128)} fusion(bf16[512,1536]{1,0:T(8,128)(2,1)} %bitcast.6, bf16[1536,1024]{1,0:T(8,128)(2,1)} %get-tuple-element.12), kind=kOutput, calls=%fused_computation.57 | convolution fusion | flops 1610612736 | bytes 6815744 | tf_op jit(solution)/shard_map/erd,edh->erh/dot_general | solution.py:166
  175.7 4.6 %fusion.23 = f32[512,1024]{1,0:T(8,128)} fusion(bf16[512,1536]{1,0:T(8,128)(2,1)} %bitcast.6, bf16[1536,1024]{1,0:T(8,128)(2,1)S(1)} %copy-done.5), kind=kOutput, calls=%fused_computation.58 | convolution fusion | flops 1610612736 | bytes 6815744 | tf_op jit(solution)/shard_map/erd,edh->erh/dot_general | solution.py:169
  180.4 7.2 %multiply_convert_fusion = (bf16[512,1024]{1,0:T(8,128)(2,1)S(1)}, bf16[512,1024]{1,0:T(8,128)(2,1)}, bf16[512,1024]{1,0:T(8,128)(2,1)S(1)}) fusion(f32[512,1024]{1,0:T(8,128)} %fusion.22, f32[512,1024]{1,0:T(8,128)} %fusion.23, bf16[512,1536]{1,0:T(8,128)(2,1)} %bitcast.18, bf16[1024,1536]{1,0:T(8,128)(2,1)} %get-tuple-element.14), kind=kOutput, calls=%fused_computation.25 | convolution fusion | flops 1618477056 | bytes 12058624 | tf_op jit(solution)/shard_map/erd,ehd->erh/dot_general | solution.py:180
  187.6 3.0 convolution_convert_fusion.2
  190.7 8.0 %all-to-all-start.1 = ((bf16[16,32,1536]{2,1,0:T(8,128)(2,1)}), bf16[16,32,1536]{2,1,0:T(8,128)(2,1)}, u32[]{:S(2)}, u32[]{:S(2)}) async-start(bf16[16,32,1536]{2,1,0:T(8,128)(2,1)} %bitcast.101), calls=%async_computation.1 | async-start | bytes 3145728 | tf_op jit(solution)/shard_map/all_to_all | solution.py:175
  198.7 5.4 %convolution_convert_fusion.1.refs_1_ = bf16[1024,1536]{1,0:T(8,128)(2,1)} fusion(bf16[512,1024]{1,0:T(8,128)(2,1)} %copy-done.10, bf16[512,1536]{1,0:T(8,128)(2,1)} %bitcast.18), kind=kOutput, calls=%fused_computation.9 | convolution fusion | flops 1612185600 | bytes 5767168 | tf_op jit(solution)/shard_map/erc,erd->cd/dot_general | solution.py:137
  204.0 1.8 fusion.24
  205.9 3.0 fusion.4
  208.9 12.7 %all-to-all-done.1 = bf16[16,32,1536]{2,1,0:T(8,128)(2,1)} async-done(((bf16[16,32,1536]{2,1,0:T(8,128)(2,1)}), bf16[16,32,1536]{2,1,0:T(8,128)(2,1)}, u32[]{:S(2)}, u32[]{:S(2)}) %all-to-all-start.1) | async-done | bytes 1572896 | tf_op jit(solution)/shard_map/all_to_all | solution.py:175
  221.6 5.1 %all-to-all-start.3 = ((bf16[16,32,1536]{2,1,0:T(8,128)(2,1)}), bf16[16,32,1536]{2,1,0:T(8,128)(2,1)}, u32[]{:S(2)}, u32[]{:S(2)}) async-start(bf16[16,32,1536]{2,1,0:T(8,128)(2,1)} %bitcast.100), calls=%async_computation.3 | async-start | bytes 3145728 | tf_op jit(solution)/shard_map/all_to_all | solution.py:190
  226.7 7.8 %convolution_convert_fusion.refs_0_ = bf16[1536,2048]{1,0:T(8,128)(2,1)} fusion(bf16[512,1536]{1,0:T(8,128)(2,1)} %bitcast.6, bf16[1,512,1024]{2,1,0:T(8,128)(2,1)S(1)} %bitcast.108, bf16[1,512,1024]{2,1,0:T(8,128)(2,1)} %bitcast.109), kind=kOutput, calls=%fused_computation.4 | convolution fusion | flops 3228565504 | bytes 9961472 | tf_op jit(solution)/shard_map/erc,erk->ck/dot_general | solution.py:134
  234.5 1.9 fusion.1
  237.4 12.4 %all-to-all-done.3 = bf16[16,32,1536]{2,1,0:T(8,128)(2,1)} async-done(((bf16[16,32,1536]{2,1,0:T(8,128)(2,1)}), bf16[16,32,1536]{2,1,0:T(8,128)(2,1)}, u32[]{:S(2)}, u32[]{:S(2)}) %all-to-all-start.3) | async-done | bytes 1572896 | tf_op jit(solution)/shard_map/all_to_all | solution.py:190
  249.7 1.8 fusion.10
  251.5 1.3 fusion.6
  254.0 4.2 all-to-all-start.4
  258.2 4.0 fusion.5
  262.1 3.8 all-to-all-done.4
  266.5 161.0 %shard_map.119 = (bf16[8,192,2048]{2,1,0:T(8,128)(2,1)}, bf16[8,128,1536]{2,1,0:T(8,128)(2,1)}, f32[8,12,128]{2,1,0:T(8,128)}) custom-call(bf16[1536,2048]{1,0:T(8,128)(2,1)} %convolution_convert_fusion.refs_0_, bf16[1024,1536]{1,0:T(8,128)(2,1)} %convolution_convert_fusion.1.refs_1_, f32[12,128]{1,0:T(8,128)} %reduce_sum.46.refs_2_), custom_call_target="tpu_custom_call" | custom-call | tf_op jit(solution)/shard_map/pallas_call | solution.py:106
  427.5 4.2 convert_reduce_fusion
  431.7 1.2 slice_bitcast_fusion
  433.6 6.3 %all-to-all-start.5 = ((f32[16,12,128]{2,1,0:T(8,128)}), f32[16,12,128]{2,1,0:T(8,128)S(1)}, u32[]{:S(2)}, u32[]{:S(2)}) async-start(f32[16,12,128]{2,1,0:T(8,128)} %broadcast_in_dim.35), calls=%async_computation.5 | async-start | bytes 262144 | tf_op jit(solution)/shard_map/all_to_all | solution.py:233
  439.9 3.3 convert_reduce_fusion.1
  443.2 4.4 all-to-all-done.5
  (56 shorter events, 7.1 us)
Async XLA Ops:
  0.6 1.2 copy-start
  4.8 8.9 %copy-start.3 = (bf16[1536,16]{0,1:T(8,128)(2,1)S(1)}, bf16[1536,16]{0,1:T(8,128)(2,1)}, u32[]{:S(2)}) copy-start(bf16[1536,16]{0,1:T(8,128)(2,1)} %param.10) | copy-start | bytes 147460
  4.8 31.7 %all-to-all-start = ((bf16[16,32,1536]{2,1,0:T(8,128)(2,1)}), bf16[16,32,1536]{2,1,0:T(8,128)(2,1)}, u32[]{:S(2)}, u32[]{:S(2)}) async-start(bf16[16,32,1536]{2,1,0:T(8,128)(2,1)} %bitcast.5), calls=%async_computation | async-start | bytes 3145728 | tf_op jit(solution)/shard_map/all_to_all | solution.py:165
  14.0 4.7 %copy-start.2 = (s32[4,16,8]{1,2,0:T(8,128)S(1)}, s32[4,16,8]{1,2,0:T(8,128)}, u32[]{:S(2)}) copy-start(s32[4,16,8]{1,2,0:T(8,128)} %param.9) | copy-start | bytes 6148
  14.0 4.8 %copy-start.1 = (bf16[256,1536]{1,0:T(8,128)(2,1)S(1)}, bf16[256,1536]{1,0:T(8,128)(2,1)}, u32[]{:S(2)}) copy-start(bf16[256,1536]{1,0:T(8,128)(2,1)} %param.8) | copy-start | bytes 2359300
  36.5 143.9 %all-to-all-start.2 = ((bf16[16,32,1536]{2,1,0:T(8,128)(2,1)}), bf16[16,32,1536]{2,1,0:T(8,128)(2,1)}, u32[]{:S(2)}, u32[]{:S(2)}) async-start(bf16[16,32,1536]{2,1,0:T(8,128)(2,1)} %fusion), calls=%async_computation.2 | async-start | bytes 3145728 | tf_op jit(solution)/shard_map/all_to_all | solution.py:178
  170.1 5.6 %copy-start.5 = (bf16[1536,1024]{1,0:T(8,128)(2,1)S(1)}, bf16[1536,1024]{1,0:T(8,128)(2,1)}, u32[]{:S(2)}) copy-start(bf16[1536,1024]{1,0:T(8,128)(2,1)} %get-tuple-element.13) | copy-start | bytes 9437188
  180.4 7.2 %copy-start.8 = (bf16[1024,1536]{1,0:T(8,128)(2,1)S(1)}, bf16[1024,1536]{1,0:T(8,128)(2,1)}, u32[]{:S(2)}) copy-start(bf16[1024,1536]{1,0:T(8,128)(2,1)} %get-tuple-element.14) | copy-start | bytes 9437188
  187.6 3.1 copy-start.10
  190.7 31.0 %all-to-all-start.1 = ((bf16[16,32,1536]{2,1,0:T(8,128)(2,1)}), bf16[16,32,1536]{2,1,0:T(8,128)(2,1)}, u32[]{:S(2)}, u32[]{:S(2)}) async-start(bf16[16,32,1536]{2,1,0:T(8,128)(2,1)} %bitcast.101), calls=%async_computation.1 | async-start | bytes 3145728 | tf_op jit(solution)/shard_map/all_to_all | solution.py:175
  198.7 5.4 %copy-start.7 = (bf16[1536,1024]{1,0:T(8,128)(2,1)S(1)}, bf16[1536,1024]{1,0:T(8,128)(2,1)}, u32[]{:S(2)}) copy-start(bf16[1536,1024]{1,0:T(8,128)(2,1)} %get-tuple-element.12) | copy-start | bytes 9437188
  198.7 5.4 %copy-start.9 = (bf16[512,1024]{1,0:T(8,128)(2,1)S(1)}, bf16[512,1024]{1,0:T(8,128)(2,1)}, u32[]{:S(2)}) copy-start(bf16[512,1024]{1,0:T(8,128)(2,1)} %get-tuple-element.45) | copy-start | bytes 3145732
  204.0 1.9 copy-start.6
  221.6 28.1 %all-to-all-start.3 = ((bf16[16,32,1536]{2,1,0:T(8,128)(2,1)}), bf16[16,32,1536]{2,1,0:T(8,128)(2,1)}, u32[]{:S(2)}, u32[]{:S(2)}) async-start(bf16[16,32,1536]{2,1,0:T(8,128)(2,1)} %bitcast.100), calls=%async_computation.3 | async-start | bytes 3145728 | tf_op jit(solution)/shard_map/all_to_all | solution.py:190
  254.0 12.0 %all-to-all-start.4 = ((f32[16,12,128]{2,1,0:T(8,128)}), f32[16,12,128]{2,1,0:T(8,128)S(1)}, u32[]{:S(2)}, u32[]{:S(2)}) async-start(f32[16,12,128]{2,1,0:T(8,128)} %reshape.191), calls=%async_computation.4 | async-start | bytes 262144 | tf_op jit(solution)/shard_map/all_to_all | solution.py:227
  431.7 1.3 copy-start.4
  433.6 14.0 %all-to-all-start.5 = ((f32[16,12,128]{2,1,0:T(8,128)}), f32[16,12,128]{2,1,0:T(8,128)S(1)}, u32[]{:S(2)}, u32[]{:S(2)}) async-start(f32[16,12,128]{2,1,0:T(8,128)} %broadcast_in_dim.35), calls=%async_computation.5 | async-start | bytes 262144 | tf_op jit(solution)/shard_map/all_to_all | solution.py:233

commit v4 on v3

--- a/solution.py
+++ b/solution.py
@@ -118,6 +118,31 @@
     return [jnp.sum(r.astype(jnp.float32), axis=0) for r in received]
 
 
+def _shift_pairs(n, k):
+    return [(i, (i + k) % n) for i in range(n)]
+
+
+def dp_gather_permute(shard, n):
+    me = lax.axis_index("dp")
+    full = jnp.zeros((n,) + shard.shape, shard.dtype)
+    full = lax.dynamic_update_index_in_dim(full, shard, me, 0)
+    for k in range(1, n):
+        got = lax.ppermute(shard, "dp", perm=_shift_pairs(n, k))
+        full = lax.dynamic_update_index_in_dim(full, got, lax.rem(me + n - k, n), 0)
+    return full
+
+
+def dp_scatter_permute(partial, n):
+    me = lax.axis_index("dp")
+    blocks = partial.reshape((n, partial.shape[0] // n) + partial.shape[1:])
+    total = lax.dynamic_index_in_dim(blocks, me, 0, keepdims=False).astype(jnp.float32)
+    for k in range(1, n):
+        piece = lax.dynamic_index_in_dim(blocks, lax.rem(me + k, n), 0, keepdims=False)
+        got = lax.ppermute(piece, "dp", perm=_shift_pairs(n, k))
+        total = total + got.astype(jnp.float32)
+    return total
+
+
 def to_blocks(slot_array, num_blocks, pick_count):
     expert_count = slot_array.shape[0]
     trailing = slot_array.shape[2:]
@@ -130,14 +155,21 @@
 
 def weight_grads(expert_rows, hidden, expert_cot, d_pre_gate, d_pre_up, router_part, n):
     hidden_activations = hidden.shape[2]
+    out_part = jnp.einsum(
+        "erc,erd->cd", hidden, expert_cot, preferred_element_type=jnp.float32
+    ).astype(jnp.bfloat16)
+    out_share = dp_scatter_permute(out_part, n)
     both_grads = jnp.concatenate([d_pre_gate, d_pre_up], axis=2)
     in_part = jnp.einsum(
         "erc,erk->ck", expert_rows, both_grads, preferred_element_type=jnp.float32
     ).astype(jnp.bfloat16)
-    out_part = jnp.einsum(
-        "erc,erd->cd", hidden, expert_cot, preferred_element_type=jnp.float32
-    ).astype(jnp.bfloat16)
-    in_share, out_share, grad_router = dp_exchange([in_part, out_part], [router_part], n)
+    in_share = dp_scatter_permute(in_part, n)
+    grad_router = jnp.sum(
+        lax.all_to_all(
+            jnp.broadcast_to(router_part[None], (n,) + router_part.shape), "dp", 0, 0, tiled=True
+        ),
+        axis=0,
+    )
     grad_gate = in_share[None, :, :hidden_activations]
     grad_up = in_share[None, :, hidden_activations:]
     down_weight_gradient = out_share[None]
@@ -158,9 +190,10 @@
     cot_rows = cotangent[slot_rows]
     scaled_cot = (slot_gate_values[:, :, None] * cot_rows.astype(jnp.float32)).astype(jnp.bfloat16)
     n = lax.axis_size("dp")
-    full_gate, full_up, full_down = (
-        g[None] for g in dp_all_gather([w_gate[0], w_up[0], w_down[0]], n)
-    )
+    gate_up = dp_gather_permute(jnp.stack([w_gate[0], w_up[0]]), n)
+    full_gate = gate_up[:, 0].reshape(1, -1, w_gate.shape[2])
+    full_up = gate_up[:, 1].reshape(1, -1, w_up.shape[2])
+    full_down = dp_gather_permute(w_down[0], n).reshape(1, -1, w_down.shape[2])
     expert_count_axis = lax.axis_size("expert")
     expert_rows = lax.all_to_all(picked, "expert", 0, 0, tiled=True).reshape(1, -1, model_width)
     pre_gate = jnp.einsum(

time: 450 us -> 408 us (0.907)
  Pallas kernels: 289 us -> 0 us
  waiting for transfers between devices: 47.2 us -> 154 us
  starting transfers between devices: 37.4 us -> 133 us
  local copies, waits for them, and re-layouts: 15.3 us -> 61.2 us
    pallas_call x2 -> x0, Pallas kernels: 289 us -> none  [the longest x1 161 us: dp_exchange(): pl.pallas_call(functools.partial(_exchange_kernel, n, len(partials)), out...]
    ppermute x0 -> x28, waiting for transfers between devices: none -> 136 us  [the longest x14 68 us: dp_scatter_permute(): got = lax.ppermute(piece, 'dp', perm=_shift_pairs(n, k))]
    ppermute x0 -> x28, starting transfers between devices: none -> 64.9 us  [the longest x14 49.2 us: dp_scatter_permute(): got = lax.ppermute(piece, 'dp', perm=_shift_pairs(n, k))]
    dynamic_update_slice x0 -> x16, local copies, waits for them, and re-layouts: none -> 21.1 us  [the longest x14 19.4 us: dp_gather_permute(): full = lax.dynamic_update_index_in_dim(full, got, lax.rem(me + n - k, n), 0)]
    all_to_all x1, starting transfers between devices: 5.06 us -> 20.5 us  [body(): lax.all_to_all(d_rows.reshape(expert_count_axis, -1, model_width), 'exper...]
    all_to_all x1, waiting for transfers between devices: 12.7 us -> 0.01 us  [body(): lax.all_to_all(expert_out.reshape(expert_count_axis, -1, model_width), 'e...]
    all_to_all x1, waiting for transfers between devices: 12.4 us -> 0.01 us  [body(): lax.all_to_all(d_rows.reshape(expert_count_axis, -1, model_width), 'exper...]
    all_to_all x0 -> x1, starting transfers between devices: none -> 8.49 us  [weight_grads(): lax.all_to_all(jnp.broadcast_to(router_part[None], (n,) + router_part.sha...]
  transfers between devices with their start and end apart: 6 -> 35, of which waited for: 5 -> 14; matrix products, arithmetic and copies ran while one was open for 11% -> 24% of each run, Pallas kernels for 29% -> 0%
where the time goes in v4:
time: 408 us; the launch traced here: 404 us
  waiting for transfers between devices  154 us (38%)
  starting transfers between devices  133 us (33%)
  local copies, waits for them, and re-layouts  61.2 us (15%)
  matrix products  44 us (11%)
  other arithmetic  11.5 us (3%)
    ppermute x14, waiting for transfers between devices, dp_scatter_permute(): got = lax.ppermute(piece, 'dp', perm=_shift_pairs(n, k))  68 us
    ppermute x14, waiting for transfers between devices, dp_gather_permute(): got = lax.ppermute(shard, 'dp', perm=_shift_pairs(n, k))  68 us
    ppermute x14, starting transfers between devices, dp_scatter_permute(): got = lax.ppermute(piece, 'dp', perm=_shift_pairs(n, k))  49.2 us
    all_to_all x1, starting transfers between devices, body(): lax.all_to_all(d_rows.reshape(expert_count_axis, -1, model_width), 'exper...  20.5 us
    dynamic_update_slice x14, local copies, waits for them, and re-layouts, dp_gather_permute(): full = lax.dynamic_update_index_in_dim(full, got, lax.rem(me + n - k, n), 0)  19.4 us
    ppermute x14, starting transfers between devices, dp_gather_permute(): got = lax.ppermute(shard, 'dp', perm=_shift_pairs(n, k))  15.8 us
    all_to_all x1, starting transfers between devices, body(): lax.all_to_all(picked, 'expert', 0, 0, tiled=True)  10.1 us
    all_to_all x1, starting transfers between devices, body(): lax.all_to_all(scaled_cot, 'expert', 0, 0, tiled=True)  9.87 us
  transfers between devices with their start and end apart: 35, of which 14 were waited for; matrix products, arithmetic and copies ran while one was open for 24% of the time, Pallas kernels for 0%

profile of v4, /device:TPU:5, one launch (start us, length us, event | category | flops | bytes accessed | tf_op | source)
XLA Modules:
  0.0 403.9 jit_solution(12934020537761337807)
XLA Ops:
  9.4 4.5 %gather_fusion.2 = f32[512]{0:T(512)S(1)} fusion(f32[16,256]{1,0:T(8,128)S(1)} %bitcast.165, s32[512]{0:T(512)S(1)} %reshape.236), kind=kCustom, calls=%fused_computation.2 | custom fusion | bytes 8192 | tf_op jit(solution)/shard_map/jit(take_along_axis)/gather | solution.py:189
  18.2 9.9 %all-to-all-start.2 = ((bf16[16,32,1536]{2,1,0:T(8,128)(2,1)}), bf16[16,32,1536]{2,1,0:T(8,128)(2,1)}, u32[]{:S(2)}, u32[]{:S(2)}) async-start(bf16[16,32,1536]{2,1,0:T(8,128)(2,1)} %fusion), calls=%async_computation.2 | async-start | bytes 3145728 | tf_op jit(solution)/shard_map/all_to_all | solution.py:211
  60.5 25.1 %collective-permute-done.13 = bf16[128,1536]{1,0:T(8,128)(2,1)S(1)} collective-permute-done((bf16[128,1536]{1,0:T(8,128)(2,1)S(1)}, bf16[128,1536]{1,0:T(8,128)(2,1)S(1)}, u32[]{:S(2)}, u32[]{:S(2)}) %collective-permute-start.13) | collective-permute-done | bytes 393248 | tf_op jit(solution)/shard_map/ppermute | solution.py:130
  86.4 10.4 %collective-permute-done = bf16[2,192,1024]{2,1,0:T(8,128)(2,1)S(1)} collective-permute-done((bf16[2,192,1024]{2,1,0:T(8,128)(2,1)S(1)}, bf16[2,192,1024]{2,1,0:T(8,128)(2,1)S(1)}, u32[]{:S(2)}, u32[]{:S(2)}) %collective-permute-start) | collective-permute-done | bytes 786464 | tf_op jit(solution)/shard_map/ppermute | solution.py:130
  102.0 22.2 %collective-permute-done.2 = bf16[2,192,1024]{2,1,0:T(8,128)(2,1)S(1)} collective-permute-done((bf16[2,192,1024]{2,1,0:T(8,128)(2,1)S(1)}, bf16[2,192,1024]{2,1,0:T(8,128)(2,1)S(1)}, u32[]{:S(2)}, u32[]{:S(2)}) %collective-permute-start.2) | collective-permute-done | bytes 786464 | tf_op jit(solution)/shard_map/ppermute | solution.py:130
  126.1 5.2 %collective-permute-done.4 = bf16[2,192,1024]{2,1,0:T(8,128)(2,1)S(1)} collective-permute-done((bf16[2,192,1024]{2,1,0:T(8,128)(2,1)S(1)}, bf16[2,192,1024]{2,1,0:T(8,128)(2,1)S(1)}, u32[]{:S(2)}, u32[]{:S(2)}) %collective-permute-start.4) | collective-permute-done | bytes 786464 | tf_op jit(solution)/shard_map/ppermute | solution.py:130
  132.3 10.1 %all-to-all-start = ((bf16[16,32,1536]{2,1,0:T(8,128)(2,1)}), bf16[16,32,1536]{2,1,0:T(8,128)(2,1)}, u32[]{:S(2)}, u32[]{:S(2)}) async-start(bf16[16,32,1536]{2,1,0:T(8,128)(2,1)} %bitcast.167), calls=%async_computation | async-start | bytes 3145728 | tf_op jit(solution)/shard_map/all_to_all | solution.py:198
  144.5 5.2 %collective-permute-done.6 = bf16[2,192,1024]{2,1,0:T(8,128)(2,1)} collective-permute-done((bf16[2,192,1024]{2,1,0:T(8,128)(2,1)S(1)}, bf16[2,192,1024]{2,1,0:T(8,128)(2,1)}, u32[]{:S(2)}, u32[]{:S(2)}) %collective-permute-start.6) | collective-permute-done | bytes 786464 | tf_op jit(solution)/shard_map/ppermute | solution.py:130
  151.7 6.5 %fusion.35 = (bf16[8,1,192,1024]{3,2,1,0:T(8,128)(2,1)}, bf16[8,1,192,1024]{3,2,1,0:T(8,128)(2,1)}) fusion(bf16[8,2,192,1024]{3,2,1,0:T(8,128)(2,1)} %bitcast_dynamic-update-slice_fusion), kind=kLoop, calls=%fused_computation.102 | loop fusion | bytes 12582912 | tf_op jit(solution)/shard_map/slice | solution.py:194
  158.2 5.5 %fusion.37 = f32[512,1024]{1,0:T(8,128)} fusion(bf16[512,1536]{1,0:T(8,128)(2,1)} %bitcast.34, bf16[1024,1536]{1,0:T(8,128)(2,1)} %bitcast.25), kind=kOutput, calls=%fused_computation.104 | convolution fusion | flops 1610612736 | bytes 6815744 | tf_op jit(solution)/shard_map/erd,ehd->erh/dot_general | solution.py:213
  163.7 6.0 %all-to-all-done = bf16[16,32,1536]{2,1,0:T(8,128)(2,1)} async-done(((bf16[16,32,1536]{2,1,0:T(8,128)(2,1)}), bf16[16,32,1536]{2,1,0:T(8,128)(2,1)}, u32[]{:S(2)}, u32[]{:S(2)}) %all-to-all-start) | async-done | bytes 1572896 | tf_op jit(solution)/shard_map/all_to_all | solution.py:198
  169.6 4.3 %fusion.36 = f32[512,1024]{1,0:T(8,128)S(1)} fusion(bf16[512,1536]{1,0:T(8,128)(2,1)} %bitcast.6, bf16[1536,1024]{1,0:T(8,128)(2,1)} %bitcast.175), kind=kOutput, calls=%fused_computation.103 | convolution fusion | flops 1610612736 | bytes 6815744 | tf_op jit(solution)/shard_map/erd,edh->erh/dot_general | solution.py:202
  174.0 4.2 %multiply_convert_fusion.1 = (bf16[512,1024]{1,0:T(8,128)(2,1)S(1)}, bf16[512,1024]{1,0:T(8,128)(2,1)S(1)}, bf16[512,1024]{1,0:T(8,128)(2,1)S(1)}) fusion(f32[512,1024]{1,0:T(8,128)S(1)} %copy-done.24, f32[512,1024]{1,0:T(8,128)S(1)} %fusion.36, bf16[512,1536]{1,0:T(8,128)(2,1)} %bitcast.6, bf16[1536,1024]{1,0:T(8,128)(2,1)S(1)} %bitcast.173), kind=kOutput, calls=%fused_computation.24 | convolution fusion | flops 1618477056 | bytes 12058624 | tf_op jit(solution)/shard_map/erd,edh->erh/dot_general | solution.py:199
  178.1 4.0 convolution_convert_fusion.1
  184.6 5.2 %convolution_convert_fusion = bf16[1536,2048]{1,0:T(8,128)(2,1)S(1)} fusion(bf16[512,1536]{1,0:T(8,128)(2,1)} %bitcast.6, bf16[1,512,1024]{2,1,0:T(8,128)(2,1)S(1)} %bitcast.189, bf16[1,512,1024]{2,1,0:T(8,128)(2,1)S(1)} %bitcast.188), kind=kOutput, calls=%fused_computation.3 | convolution fusion | flops 3228565504 | bytes 9961472 | tf_op jit(solution)/shard_map/erc,erk->ck/dot_general | solution.py:163
  200.6 4.9 %convolution_convert_fusion.2 = bf16[512,1536]{1,0:T(8,128)(2,1)} fusion(bf16[512,1024]{1,0:T(8,128)(2,1)S(1)} %get-tuple-element.55, bf16[1024,1536]{1,0:T(8,128)(2,1)} %bitcast.25), kind=kOutput, calls=%fused_computation.15 | convolution fusion | flops 1611399168 | bytes 5767168 | tf_op jit(solution)/shard_map/erh,ehd->erd/dot_general | solution.py:205
  205.5 6.5 %all-to-all-start.1 = ((bf16[16,32,1536]{2,1,0:T(8,128)(2,1)}), bf16[16,32,1536]{2,1,0:T(8,128)(2,1)}, u32[]{:S(2)}, u32[]{:S(2)}) async-start(bf16[16,32,1536]{2,1,0:T(8,128)(2,1)} %bitcast.177), calls=%async_computation.1 | async-start | bytes 3145728 | tf_op jit(solution)/shard_map/all_to_all | solution.py:208
  212.0 36.6 %collective-permute-done.26 = bf16[128,1536]{1,0:T(8,128)(2,1)} collective-permute-done((bf16[128,1536]{1,0:T(8,128)(2,1)}, bf16[128,1536]{1,0:T(8,128)(2,1)}, u32[]{:S(2)}, u32[]{:S(2)}) %collective-permute-start.26) | collective-permute-done | bytes 393248 | tf_op jit(solution)/shard_map/ppermute | solution.py:141
  248.5 11.1 %collective-permute-start.22 = (bf16[128,1536]{1,0:T(8,128)(2,1)}, bf16[128,1536]{1,0:T(8,128)(2,1)S(1)}, u32[]{:S(2)}, u32[]{:S(2)}) collective-permute-start(bf16[128,1536]{1,0:T(8,128)(2,1)} %get-tuple-element.62), channel_id=1, source_target_pairs={{0,32},{16,48},{32,64},{48,80},{64,96},{80,112},{96,0},{112,16},{1... | collective-permute-start | bytes 1179656 | tf_op jit(solution)/shard_map/ppermute | solution.py:141
  263.0 4.0 fusion.38
  267.1 9.9 %collective-permute-start.18 = (bf16[192,2048]{1,0:T(8,128)(2,1)}, bf16[192,2048]{1,0:T(8,128)(2,1)}, u32[]{:S(2)}, u32[]{:S(2)}) collective-permute-start(bf16[192,2048]{1,0:T(8,128)(2,1)} %get-tuple-element.47), channel_id=1, source_target_pairs={{0,80},{16,96},{32,112},{48,0},{64,16},{80,32},{96,48},{112,64},{1... | collective-permute-start | bytes 2359304 | tf_op jit(solution)/shard_map/ppermute | solution.py:141
  279.6 4.1 %collective-permute-start.15 = (bf16[192,2048]{1,0:T(8,128)(2,1)}, bf16[192,2048]{1,0:T(8,128)(2,1)}, u32[]{:S(2)}, u32[]{:S(2)}) collective-permute-start(bf16[192,2048]{1,0:T(8,128)(2,1)} %get-tuple-element.50), channel_id=1, source_target_pairs={{0,32},{16,48},{32,64},{48,80},{64,96},{80,112},{96,0},{112,16},{1... | collective-permute-start | bytes 2359304 | tf_op jit(solution)/shard_map/ppermute | solution.py:141
  283.7 13.9 %collective-permute-start.14 = (bf16[192,2048]{1,0:T(8,128)(2,1)S(1)}, bf16[192,2048]{1,0:T(8,128)(2,1)}, u32[]{:S(2)}, u32[]{:S(2)}) collective-permute-start(bf16[192,2048]{1,0:T(8,128)(2,1)S(1)} %get-tuple-element.44), channel_id=1, source_target_pairs={{0,16},{16,32},{32,48},{48,64},{64,80},{80,96},{96,112},{112,0},{1... | collective-permute-start | bytes 2359304 | tf_op jit(solution)/shard_map/ppermute | solution.py:141
  303.3 20.5 %all-to-all-start.3 = ((bf16[16,32,1536]{2,1,0:T(8,128)(2,1)}), bf16[16,32,1536]{2,1,0:T(8,128)(2,1)}, u32[]{:S(2)}, u32[]{:S(2)}) async-start(bf16[16,32,1536]{2,1,0:T(8,128)(2,1)} %bitcast.178), calls=%async_computation.3 | async-start | bytes 3145728 | tf_op jit(solution)/shard_map/all_to_all | solution.py:223
  325.7 20.3 %collective-permute-done.15 = bf16[192,2048]{1,0:T(8,128)(2,1)} collective-permute-done((bf16[192,2048]{1,0:T(8,128)(2,1)}, bf16[192,2048]{1,0:T(8,128)(2,1)}, u32[]{:S(2)}, u32[]{:S(2)}) %collective-permute-start.15) | collective-permute-done | bytes 786464 | tf_op jit(solution)/shard_map/ppermute | solution.py:141
  346.1 6.7 %collective-permute-done.14 = bf16[192,2048]{1,0:T(8,128)(2,1)} collective-permute-done((bf16[192,2048]{1,0:T(8,128)(2,1)S(1)}, bf16[192,2048]{1,0:T(8,128)(2,1)}, u32[]{:S(2)}, u32[]{:S(2)}) %collective-permute-start.14) | collective-permute-done | bytes 786464 | tf_op jit(solution)/shard_map/ppermute | solution.py:141
  352.7 3.9 fusion.15
  362.0 6.9 %all-to-all-start.4 = ((f32[16,12,128]{2,1,0:T(8,128)}), f32[16,12,128]{2,1,0:T(8,128)S(1)}, u32[]{:S(2)}, u32[]{:S(2)}) async-start(f32[16,12,128]{2,1,0:T(8,128)} %reshape.214), calls=%async_computation.4 | async-start | bytes 262144 | tf_op jit(solution)/shard_map/all_to_all | solution.py:260
  370.7 5.9 %all-to-all-done.4 = f32[16,12,128]{2,1,0:T(8,128)S(1)} async-done(((f32[16,12,128]{2,1,0:T(8,128)}), f32[16,12,128]{2,1,0:T(8,128)S(1)}, u32[]{:S(2)}, u32[]{:S(2)}) %all-to-all-start.4) | async-done | bytes 98336 | tf_op jit(solution)/shard_map/all_to_all | solution.py:260
  377.2 8.5 %all-to-all-start.5 = ((f32[8,12,128]{2,1,0:T(8,128)}), f32[8,12,128]{2,1,0:T(8,128)S(1)}, u32[]{:S(2)}, u32[]{:S(2)}) async-start(f32[8,12,128]{2,1,0:T(8,128)} %broadcast_in_dim.109), calls=%async_computation.5 | async-start | bytes 131072 | tf_op jit(solution)/shard_map/all_to_all | solution.py:168
  389.6 5.4 %all-to-all-start.6 = ((f32[16,12,128]{2,1,0:T(8,128)}), f32[16,12,128]{2,1,0:T(8,128)S(1)}, u32[]{:S(2)}, u32[]{:S(2)}) async-start(f32[16,12,128]{2,1,0:T(8,128)} %broadcast_in_dim.110), calls=%async_computation.6 | async-start | bytes 262144 | tf_op jit(solution)/shard_map/all_to_all | solution.py:266
  395.0 4.0 fusion.5
  (164 shorter events, 101.8 us)
Async XLA Ops:
  0.6 44.5 %collective-permute-start.7 = (bf16[128,1536]{1,0:T(8,128)(2,1)}, bf16[128,1536]{1,0:T(8,128)(2,1)}, u32[]{:S(2)}, u32[]{:S(2)}) collective-permute-start(bf16[128,1536]{1,0:T(8,128)(2,1)} %bitcast.179), channel_id=1, source_target_pairs={{0,16},{16,32},{32,48},{48,64},{64,80},{80,96},{96,112},{112,0},{1... | collective-permute-start | bytes 1179656 | tf_op jit(solution)/shard_map/ppermute | solution.py:130
  2.0 45.8 %collective-permute-start.8 = (bf16[128,1536]{1,0:T(8,128)(2,1)}, bf16[128,1536]{1,0:T(8,128)(2,1)}, u32[]{:S(2)}, u32[]{:S(2)}) collective-permute-start(bf16[128,1536]{1,0:T(8,128)(2,1)} %bitcast.180), channel_id=1, source_target_pairs={{0,32},{16,48},{32,64},{48,80},{64,96},{80,112},{96,0},{112,16},{1... | collective-permute-start | bytes 1179656 | tf_op jit(solution)/shard_map/ppermute | solution.py:130
  2.9 47.1 %collective-permute-start.9 = (bf16[128,1536]{1,0:T(8,128)(2,1)}, bf16[128,1536]{1,0:T(8,128)(2,1)}, u32[]{:S(2)}, u32[]{:S(2)}) collective-permute-start(bf16[128,1536]{1,0:T(8,128)(2,1)} %bitcast.181), channel_id=1, source_target_pairs={{0,48},{16,64},{32,80},{48,96},{64,112},{80,0},{96,16},{112,32},{1... | collective-permute-start | bytes 1179656 | tf_op jit(solution)/shard_map/ppermute | solution.py:130
  3.9 48.9 %collective-permute-start.10 = (bf16[128,1536]{1,0:T(8,128)(2,1)}, bf16[128,1536]{1,0:T(8,128)(2,1)}, u32[]{:S(2)}, u32[]{:S(2)}) collective-permute-start(bf16[128,1536]{1,0:T(8,128)(2,1)} %bitcast.182), channel_id=1, source_target_pairs={{0,64},{16,80},{32,96},{48,112},{64,0},{80,16},{96,32},{112,48},{1... | collective-permute-start | bytes 1179656 | tf_op jit(solution)/shard_map/ppermute | solution.py:130
  5.2 50.4 %collective-permute-start.11 = (bf16[128,1536]{1,0:T(8,128)(2,1)}, bf16[128,1536]{1,0:T(8,128)(2,1)}, u32[]{:S(2)}, u32[]{:S(2)}) collective-permute-start(bf16[128,1536]{1,0:T(8,128)(2,1)} %bitcast.183), channel_id=1, source_target_pairs={{0,80},{16,96},{32,112},{48,0},{64,16},{80,32},{96,48},{112,64},{1... | collective-permute-start | bytes 1179656 | tf_op jit(solution)/shard_map/ppermute | solution.py:130
  18.2 114.1 %all-to-all-start.2 = ((bf16[16,32,1536]{2,1,0:T(8,128)(2,1)}), bf16[16,32,1536]{2,1,0:T(8,128)(2,1)}, u32[]{:S(2)}, u32[]{:S(2)}) async-start(bf16[16,32,1536]{2,1,0:T(8,128)(2,1)} %fusion), calls=%async_computation.2 | async-start | bytes 3145728 | tf_op jit(solution)/shard_map/all_to_all | solution.py:211
  45.1 14.6 %collective-permute-start.12 = (bf16[128,1536]{1,0:T(8,128)(2,1)S(1)}, bf16[128,1536]{1,0:T(8,128)(2,1)S(1)}, u32[]{:S(2)}, u32[]{:S(2)}) collective-permute-start(bf16[128,1536]{1,0:T(8,128)(2,1)S(1)} %bitcast.184), channel_id=1, source_target_pairs={{0,96},{16,112},{32,0},{48,16},{64,32},{80,48},{96,64},{112,80},{1... | collective-permute-start | bytes 1179656 | tf_op jit(solution)/shard_map/ppermute | solution.py:130
  47.8 37.8 %collective-permute-start.13 = (bf16[128,1536]{1,0:T(8,128)(2,1)S(1)}, bf16[128,1536]{1,0:T(8,128)(2,1)S(1)}, u32[]{:S(2)}, u32[]{:S(2)}) collective-permute-start(bf16[128,1536]{1,0:T(8,128)(2,1)S(1)} %bitcast.185), channel_id=1, source_target_pairs={{0,112},{16,0},{32,16},{48,32},{64,48},{80,64},{96,80},{112,96},{1... | collective-permute-start | bytes 1179656 | tf_op jit(solution)/shard_map/ppermute | solution.py:130
  50.0 46.7 %collective-permute-start = (bf16[2,192,1024]{2,1,0:T(8,128)(2,1)S(1)}, bf16[2,192,1024]{2,1,0:T(8,128)(2,1)S(1)}, u32[]{:S(2)}, u32[]{:S(2)}) collective-permute-start(bf16[2,192,1024]{2,1,0:T(8,128)(2,1)S(1)} %constant_dynamic-update-slice_fusion.1), channel_id=1, source_target_pairs={{0,16},{16,32},{32,48},{48,64},{64,80},{80,96},{96,112},{112,0},{1... | collective-permute-start | bytes 2359304 | tf_op jit(solution)/shard_map/ppermute | solution.py:130
  52.8 44.8 %collective-permute-start.1 = (bf16[2,192,1024]{2,1,0:T(8,128)(2,1)S(1)}, bf16[2,192,1024]{2,1,0:T(8,128)(2,1)S(1)}, u32[]{:S(2)}, u32[]{:S(2)}) collective-permute-start(bf16[2,192,1024]{2,1,0:T(8,128)(2,1)S(1)} %constant_dynamic-update-slice_fusion.1), channel_id=1, source_target_pairs={{0,32},{16,48},{32,64},{48,80},{64,96},{80,112},{96,0},{112,16},{1... | collective-permute-start | bytes 2359304 | tf_op jit(solution)/shard_map/ppermute | solution.py:130
  55.5 68.6 %collective-permute-start.2 = (bf16[2,192,1024]{2,1,0:T(8,128)(2,1)S(1)}, bf16[2,192,1024]{2,1,0:T(8,128)(2,1)S(1)}, u32[]{:S(2)}, u32[]{:S(2)}) collective-permute-start(bf16[2,192,1024]{2,1,0:T(8,128)(2,1)S(1)} %constant_dynamic-update-slice_fusion.1), channel_id=1, source_target_pairs={{0,48},{16,64},{32,80},{48,96},{64,112},{80,0},{96,16},{112,32},{1... | collective-permute-start | bytes 2359304 | tf_op jit(solution)/shard_map/ppermute | solution.py:130
  59.7 65.5 %collective-permute-start.3 = (bf16[2,192,1024]{2,1,0:T(8,128)(2,1)S(1)}, bf16[2,192,1024]{2,1,0:T(8,128)(2,1)S(1)}, u32[]{:S(2)}, u32[]{:S(2)}) collective-permute-start(bf16[2,192,1024]{2,1,0:T(8,128)(2,1)S(1)} %constant_dynamic-update-slice_fusion.1), channel_id=1, source_target_pairs={{0,64},{16,80},{32,96},{48,112},{64,0},{80,16},{96,32},{112,48},{1... | collective-permute-start | bytes 2359304 | tf_op jit(solution)/shard_map/ppermute | solution.py:130
  85.6 45.7 %collective-permute-start.4 = (bf16[2,192,1024]{2,1,0:T(8,128)(2,1)S(1)}, bf16[2,192,1024]{2,1,0:T(8,128)(2,1)S(1)}, u32[]{:S(2)}, u32[]{:S(2)}) collective-permute-start(bf16[2,192,1024]{2,1,0:T(8,128)(2,1)S(1)} %constant_dynamic-update-slice_fusion.1), channel_id=1, source_target_pairs={{0,80},{16,96},{32,112},{48,0},{64,16},{80,32},{96,48},{112,64},{1... | collective-permute-start | bytes 2359304 | tf_op jit(solution)/shard_map/ppermute | solution.py:130
  96.7 45.7 %collective-permute-start.5 = (bf16[2,192,1024]{2,1,0:T(8,128)(2,1)S(1)}, bf16[2,192,1024]{2,1,0:T(8,128)(2,1)}, u32[]{:S(2)}, u32[]{:S(2)}) collective-permute-start(bf16[2,192,1024]{2,1,0:T(8,128)(2,1)S(1)} %constant_dynamic-update-slice_fusion.1), channel_id=1, source_target_pairs={{0,96},{16,112},{32,0},{48,16},{64,32},{80,48},{96,64},{112,80},{1... | collective-permute-start | bytes 2359304 | tf_op jit(solution)/shard_map/ppermute | solution.py:130
  97.6 52.0 %collective-permute-start.6 = (bf16[2,192,1024]{2,1,0:T(8,128)(2,1)S(1)}, bf16[2,192,1024]{2,1,0:T(8,128)(2,1)}, u32[]{:S(2)}, u32[]{:S(2)}) collective-permute-start(bf16[2,192,1024]{2,1,0:T(8,128)(2,1)S(1)} %constant_dynamic-update-slice_fusion.1), channel_id=1, source_target_pairs={{0,112},{16,0},{32,16},{48,32},{64,48},{80,64},{96,80},{112,96},{1... | collective-permute-start | bytes 2359304 | tf_op jit(solution)/shard_map/ppermute | solution.py:130
  132.3 37.3 %all-to-all-start = ((bf16[16,32,1536]{2,1,0:T(8,128)(2,1)}), bf16[16,32,1536]{2,1,0:T(8,128)(2,1)}, u32[]{:S(2)}, u32[]{:S(2)}) async-start(bf16[16,32,1536]{2,1,0:T(8,128)(2,1)} %bitcast.167), calls=%async_computation | async-start | bytes 3145728 | tf_op jit(solution)/shard_map/all_to_all | solution.py:198
  183.7 16.2 %collective-permute-start.27 = (bf16[128,1536]{1,0:T(8,128)(2,1)S(1)}, bf16[128,1536]{1,0:T(8,128)(2,1)S(1)}, u32[]{:S(2)}, u32[]{:S(2)}) collective-permute-start(bf16[128,1536]{1,0:T(8,128)(2,1)S(1)} %get-tuple-element.57), channel_id=1, source_target_pairs={{0,112},{16,0},{32,16},{48,32},{64,48},{80,64},{96,80},{112,96},{1... | collective-permute-start | bytes 1179656 | tf_op jit(solution)/shard_map/ppermute | solution.py:141
  193.9 85.7 %collective-permute-start.20 = (bf16[192,2048]{1,0:T(8,128)(2,1)}, bf16[192,2048]{1,0:T(8,128)(2,1)}, u32[]{:S(2)}, u32[]{:S(2)}) collective-permute-start(bf16[192,2048]{1,0:T(8,128)(2,1)} %get-tuple-element.45), channel_id=1, source_target_pairs={{0,112},{16,0},{32,16},{48,32},{64,48},{80,64},{96,80},{112,96},{1... | collective-permute-start | bytes 2359304 | tf_op jit(solution)/shard_map/ppermute | solution.py:141
  195.3 88.3 %collective-permute-start.19 = (bf16[192,2048]{1,0:T(8,128)(2,1)}, bf16[192,2048]{1,0:T(8,128)(2,1)}, u32[]{:S(2)}, u32[]{:S(2)}) collective-permute-start(bf16[192,2048]{1,0:T(8,128)(2,1)} %get-tuple-element.46), channel_id=1, source_target_pairs={{0,96},{16,112},{32,0},{48,16},{64,32},{80,48},{96,64},{112,80},{1... | collective-permute-start | bytes 2359304 | tf_op jit(solution)/shard_map/ppermute | solution.py:141
  197.3 51.3 %collective-permute-start.26 = (bf16[128,1536]{1,0:T(8,128)(2,1)}, bf16[128,1536]{1,0:T(8,128)(2,1)}, u32[]{:S(2)}, u32[]{:S(2)}) collective-permute-start(bf16[128,1536]{1,0:T(8,128)(2,1)} %get-tuple-element.58), channel_id=1, source_target_pairs={{0,96},{16,112},{32,0},{48,16},{64,32},{80,48},{96,64},{112,80},{1... | collective-permute-start | bytes 1179656 | tf_op jit(solution)/shard_map/ppermute | solution.py:141
  198.2 50.4 %collective-permute-start.25 = (bf16[128,1536]{1,0:T(8,128)(2,1)}, bf16[128,1536]{1,0:T(8,128)(2,1)}, u32[]{:S(2)}, u32[]{:S(2)}) collective-permute-start(bf16[128,1536]{1,0:T(8,128)(2,1)} %get-tuple-element.59), channel_id=1, source_target_pairs={{0,80},{16,96},{32,112},{48,0},{64,16},{80,32},{96,48},{112,64},{1... | collective-permute-start | bytes 1179656 | tf_op jit(solution)/shard_map/ppermute | solution.py:141
  199.9 59.7 %collective-permute-start.24 = (bf16[128,1536]{1,0:T(8,128)(2,1)}, bf16[128,1536]{1,0:T(8,128)(2,1)}, u32[]{:S(2)}, u32[]{:S(2)}) collective-permute-start(bf16[128,1536]{1,0:T(8,128)(2,1)} %get-tuple-element.60), channel_id=1, source_target_pairs={{0,64},{16,80},{32,96},{48,112},{64,0},{80,16},{96,32},{112,48},{1... | collective-permute-start | bytes 1179656 | tf_op jit(solution)/shard_map/ppermute | solution.py:141
  205.5 97.7 %all-to-all-start.1 = ((bf16[16,32,1536]{2,1,0:T(8,128)(2,1)}), bf16[16,32,1536]{2,1,0:T(8,128)(2,1)}, u32[]{:S(2)}, u32[]{:S(2)}) async-start(bf16[16,32,1536]{2,1,0:T(8,128)(2,1)} %bitcast.177), calls=%async_computation.1 | async-start | bytes 3145728 | tf_op jit(solution)/shard_map/all_to_all | solution.py:208
  248.5 18.5 %collective-permute-start.23 = (bf16[128,1536]{1,0:T(8,128)(2,1)}, bf16[128,1536]{1,0:T(8,128)(2,1)S(1)}, u32[]{:S(2)}, u32[]{:S(2)}) collective-permute-start(bf16[128,1536]{1,0:T(8,128)(2,1)} %get-tuple-element.61), channel_id=1, source_target_pairs={{0,48},{16,64},{32,80},{48,96},{64,112},{80,0},{96,16},{112,32},{1... | collective-permute-start | bytes 1179656 | tf_op jit(solution)/shard_map/ppermute | solution.py:141
  248.5 28.4 %collective-permute-start.22 = (bf16[128,1536]{1,0:T(8,128)(2,1)}, bf16[128,1536]{1,0:T(8,128)(2,1)S(1)}, u32[]{:S(2)}, u32[]{:S(2)}) collective-permute-start(bf16[128,1536]{1,0:T(8,128)(2,1)} %get-tuple-element.62), channel_id=1, source_target_pairs={{0,32},{16,48},{32,64},{48,80},{64,96},{80,112},{96,0},{112,16},{1... | collective-permute-start | bytes 1179656 | tf_op jit(solution)/shard_map/ppermute | solution.py:141
  259.6 19.9 %collective-permute-start.21 = (bf16[128,1536]{1,0:T(8,128)(2,1)}, bf16[128,1536]{1,0:T(8,128)(2,1)S(1)}, u32[]{:S(2)}, u32[]{:S(2)}) collective-permute-start(bf16[128,1536]{1,0:T(8,128)(2,1)} %get-tuple-element.56), channel_id=1, source_target_pairs={{0,16},{16,32},{32,48},{48,64},{64,80},{80,96},{96,112},{112,0},{1... | collective-permute-start | bytes 1179656 | tf_op jit(solution)/shard_map/ppermute | solution.py:141
  267.1 56.7 %collective-permute-start.18 = (bf16[192,2048]{1,0:T(8,128)(2,1)}, bf16[192,2048]{1,0:T(8,128)(2,1)}, u32[]{:S(2)}, u32[]{:S(2)}) collective-permute-start(bf16[192,2048]{1,0:T(8,128)(2,1)} %get-tuple-element.47), channel_id=1, source_target_pairs={{0,80},{16,96},{32,112},{48,0},{64,16},{80,32},{96,48},{112,64},{1... | collective-permute-start | bytes 2359304 | tf_op jit(solution)/shard_map/ppermute | solution.py:141
  277.0 46.8 %collective-permute-start.17 = (bf16[192,2048]{1,0:T(8,128)(2,1)}, bf16[192,2048]{1,0:T(8,128)(2,1)}, u32[]{:S(2)}, u32[]{:S(2)}) collective-permute-start(bf16[192,2048]{1,0:T(8,128)(2,1)} %get-tuple-element.48), channel_id=1, source_target_pairs={{0,64},{16,80},{32,96},{48,112},{64,0},{80,16},{96,32},{112,48},{1... | collective-permute-start | bytes 2359304 | tf_op jit(solution)/shard_map/ppermute | solution.py:141
  279.6 46.2 %collective-permute-start.16 = (bf16[192,2048]{1,0:T(8,128)(2,1)}, bf16[192,2048]{1,0:T(8,128)(2,1)}, u32[]{:S(2)}, u32[]{:S(2)}) collective-permute-start(bf16[192,2048]{1,0:T(8,128)(2,1)} %get-tuple-element.49), channel_id=1, source_target_pairs={{0,48},{16,64},{32,80},{48,96},{64,112},{80,0},{96,16},{112,32},{1... | collective-permute-start | bytes 2359304 | tf_op jit(solution)/shard_map/ppermute | solution.py:141
  279.6 66.5 %collective-permute-start.15 = (bf16[192,2048]{1,0:T(8,128)(2,1)}, bf16[192,2048]{1,0:T(8,128)(2,1)}, u32[]{:S(2)}, u32[]{:S(2)}) collective-permute-start(bf16[192,2048]{1,0:T(8,128)(2,1)} %get-tuple-element.50), channel_id=1, source_target_pairs={{0,32},{16,48},{32,64},{48,80},{64,96},{80,112},{96,0},{112,16},{1... | collective-permute-start | bytes 2359304 | tf_op jit(solution)/shard_map/ppermute | solution.py:141
  283.7 69.1 %collective-permute-start.14 = (bf16[192,2048]{1,0:T(8,128)(2,1)S(1)}, bf16[192,2048]{1,0:T(8,128)(2,1)}, u32[]{:S(2)}, u32[]{:S(2)}) collective-permute-start(bf16[192,2048]{1,0:T(8,128)(2,1)S(1)} %get-tuple-element.44), channel_id=1, source_target_pairs={{0,16},{16,32},{32,48},{48,64},{64,80},{80,96},{96,112},{112,0},{1... | collective-permute-start | bytes 2359304 | tf_op jit(solution)/shard_map/ppermute | solution.py:141
  303.3 58.7 %all-to-all-start.3 = ((bf16[16,32,1536]{2,1,0:T(8,128)(2,1)}), bf16[16,32,1536]{2,1,0:T(8,128)(2,1)}, u32[]{:S(2)}, u32[]{:S(2)}) async-start(bf16[16,32,1536]{2,1,0:T(8,128)(2,1)} %bitcast.178), calls=%async_computation.3 | async-start | bytes 3145728 | tf_op jit(solution)/shard_map/all_to_all | solution.py:223
  (28 other events, 308.5 us)
